TPU v7x, 128 devices: a whole 4x4x4 slice. The times are simulated.
128 devices in a mesh: wide: 16 (over z, x), narrow: 8 (over y, core).
Axes of the slice: x: 4, y: 4, z: 4, core: 2. Of those that a mesh axis runs over, the one named last changes fastest.
Arguments:
- recording: bfloat16 [131072, 512], P(('wide', 'narrow')), may hold values from -6 to 6
- conv_weight: bfloat16 [3, 3, 512, 512], replicated, may hold values from -0.15625 to 0.15625
- conv_bias: float32 [3, 512], replicated, may hold values from -3 to 3
- projection: bfloat16 [512, 64], replicated, may hold values from -0.25 to 0.25
Outputs:
- path_points: bfloat16 [131072, 64], P(('wide', 'narrow'))
- level_one: float32 [16, 64], P('wide')
- level_two: float32 [16, 4096], P('wide')
- level_three: float32 [16, 64, 4096], P('wide', 'narrow')
All inputs are finite; a program needn't handle non-finite values.
Results may differ from a plain program's by a relative error of at most 0.0075.
Values may be sent and summed in bfloat16 or wider, within the bound.
A program may use at most 64 MiB of HBM per device.

v0:
```python
import jax
import jax.numpy as jnp
from jax import lax
from jax.sharding import Mesh
from jax.sharding import PartitionSpec as P

WIDE = ("wide_0", "wide_1")
WIDE_NARROW = ("wide_0", "wide_1", "narrow")


PRECISE = lax.Precision.HIGHEST


def padded_2(array, sides, width):
    for axis, dim in sides:
        size, length = (lax.axis_size(axis), array.shape[dim])
        up = [(i, (i + 1) % size) for i in range(size - 1)]
        down = [(j, i) for i, j in up]
        last = lax.slice_in_dim(array, length - width, length, axis=dim)
        first = lax.slice_in_dim(array, 0, width, axis=dim)
        before = lax.ppermute(last, axis, up)
        after = lax.ppermute(first, axis, down)
        array = jnp.concatenate([before, array, after], axis=dim)
    return array


def from_behind(array, axis, by):
    size = lax.axis_size(axis)
    pairs = [(i, i + by) for i in range(size) if 0 <= i + by < size]
    return lax.ppermute(array, axis, pairs)


def in_one_piece(arrays, axis, dim, along):
    columns = [a.reshape(*a.shape[:along], -1) for a in arrays]
    both = jnp.concatenate(columns, axis=along)
    result, at, gathered = (lax.all_gather(both, axis, axis=dim, tiled=True), 0, [])
    for a, column in zip(arrays, columns):
        slab = result[..., at : at + column.shape[along]]
        gathered.append(slab.reshape(*slab.shape[:along], *a.shape[along:]))
        at += column.shape[along]
    return tuple(gathered)


def neutral_like(array, identity):
    return jax.tree.map(
        lambda part, zero: jnp.zeros_like(part) + jnp.asarray(zero, part.dtype), array, identity
    )


def all_in_one(array, axis):
    leaves = jax.tree.leaves(array)
    turns = sorted(range(len(leaves)), key=lambda k: -leaves[k].size)
    width = (1, *leaves[turns[0]].shape)[-1]
    lines = [
        jnp.pad(leaves[k].reshape(-1), (0, -leaves[k].size % width)).reshape(-1, width)
        for k in turns
    ]
    both, at, found = (lax.all_gather(jnp.concatenate(lines), axis), 0, {})
    for k, line in zip(turns, lines):
        slab = both[:, at : at + len(line)].reshape(len(both), -1)
        found[k] = slab[:, : leaves[k].size].reshape(-1, *leaves[k].shape)
        at += len(line)
    numbers = iter(range(len(leaves)))
    return jax.tree.map(lambda _: found[next(numbers)], array)


def entering(array, axes, combine, identity):
    before = start = neutral_like(array, identity)
    running = array
    for axis in reversed(axes):
        size, index = (lax.axis_size(axis), lax.axis_index(axis))
        pieces = all_in_one(running, axis)
        inside, running = (start, start)
        for k in range(size):
            passed = k < index
            running = combine(running, jax.tree.map(lambda part: part[k], pieces))
            inside = jax.tree.map(lambda new, old: jnp.where(passed, new, old), running, inside)
        before = combine(inside, before)
    return before


def apply_taps(padded, weights, layer_bias, dilation, length):
    totals = layer_bias[None, :]
    for tap_idx in range(3):
        window = padded[tap_idx * dilation : tap_idx * dilation + length]
        totals = totals + jnp.dot(window, weights[tap_idx], preferred_element_type=jnp.float32)
    return totals


def sig_update(signature, increments, row_count):
    first_level, second_level, third_level = signature
    path_width = increments.shape[1]
    step_count = increments.shape[0]
    running = jnp.cumsum(increments, axis=0)
    totals = running[-1]
    before = first_level[None, :] + running - increments
    remaining = totals[None, :] - running
    second_terms = ((before + 0.5 * increments)[:, :, None] * increments[:, None, :]).reshape(
        step_count, row_count * path_width
    )
    third_terms = ((0.5 * before + increments / 6.0)[:, :, None] * increments[:, None, :]).reshape(
        step_count, row_count * path_width
    )
    gained = jnp.einsum("nm,nk->mk", second_terms, remaining, precision=PRECISE)
    gained = gained + jnp.einsum("nm,nk->mk", third_terms, increments, precision=PRECISE)
    second_rows = second_level
    carried = (second_rows[:, :, None] * totals[None, None, :]).reshape(
        row_count, path_width * path_width
    )
    third_level = third_level + carried + gained.reshape(row_count, path_width * path_width)
    second_level = second_level + jnp.einsum("ni,nj->ij", before, increments, precision=PRECISE)
    second_level = second_level + 0.5 * jnp.einsum(
        "ni,nj->ij", increments, increments, precision=PRECISE
    )
    first_level = first_level + totals
    return (first_level, second_level, third_level)


def chen(earlier, later, row_start, row_count):
    first_a, second_a, third_a = earlier
    first_b, second_b, third_b = later
    first_level = first_a + first_b
    second_level = second_a + second_b + first_a[:, None] * first_b[None, :]
    first_rows = lax.dynamic_slice_in_dim(first_a, row_start, row_count, 0)
    second_rows = lax.dynamic_slice_in_dim(second_a, row_start, row_count, 0)
    mixed = first_rows[:, None] * second_b.reshape(1, -1)
    mixed = mixed + (second_rows[:, :, None] * first_b[None, None, :]).reshape(row_count, -1)
    return (first_level, second_level, third_a + third_b + mixed)


def per_device(recording, conv_weight, conv_bias, projection):
    shard_len = recording.shape[0]
    layers = conv_weight.shape[0]
    path_width = projection.shape[1]
    narrow_size = lax.axis_size("narrow")
    total_steps = shard_len * lax.axis_size(WIDE) * narrow_size
    reach_cells = 2**layers - 1
    padded = padded_2(recording, ((WIDE_NARROW, 0),), reach_cells)
    anchor = (
        lax.axis_index(WIDE) * narrow_size + lax.axis_index("narrow")
    ) * shard_len - reach_cells
    for layer_idx in range(layers):
        dilation = 2**layer_idx
        length = padded.shape[0] - 2 * dilation
        totals = apply_taps(padded, conv_weight[layer_idx], conv_bias[layer_idx], dilation, length)
        updated = (
            padded[dilation : dilation + length].astype(jnp.float32) + jax.nn.silu(totals)
        ).astype(jnp.bfloat16)
        anchor = anchor + dilation
        position = anchor + jnp.arange(length, dtype=jnp.int32)
        inside = (position >= 0) & (position < total_steps)
        padded = jnp.where(inside[:, None], updated, jnp.zeros_like(updated))
    path_points = jnp.dot(padded, projection, preferred_element_type=jnp.float32).astype(
        jnp.bfloat16
    )
    step_scale = total_steps ** (-0.2)
    row_count = path_width // narrow_size
    row_start = lax.axis_index("narrow") * row_count
    empty_state = (
        jnp.zeros((path_width,), jnp.float32),
        jnp.zeros((path_width, path_width), jnp.float32),
        jnp.zeros((row_count, path_width * path_width), jnp.float32),
    )

    def combine(earlier, later):
        return chen(earlier, later, row_start, row_count)

    previous = from_behind(path_points[-1:], WIDE_NARROW, 1)
    own_points = jnp.concatenate([previous, path_points], axis=0).astype(jnp.float32)
    own_steps = (own_points[1:] - own_points[:-1]) * step_scale
    quarters = own_steps.reshape(4, shard_len // 4, path_width)
    whole_empty = (
        empty_state[0],
        empty_state[1],
        jnp.zeros((path_width, path_width * path_width), jnp.float32),
    )

    def whole_step(signature, piece):
        return (sig_update(signature, piece, path_width), None)

    partial_sig, unused = lax.scan(whole_step, whole_empty, quarters)
    third_parts = lax.all_to_all(
        partial_sig[2].reshape(1, path_width, path_width * path_width).astype(jnp.bfloat16),
        "narrow",
        split_axis=1,
        concat_axis=0,
        tiled=True,
    ).astype(jnp.float32)
    first_parts, second_parts = in_one_piece(
        (partial_sig[0][None], partial_sig[1][None]), "narrow", 0, 2
    )

    def fold_step(signature, element):
        return (combine(signature, element), None)

    signature, unused = lax.scan(fold_step, empty_state, (first_parts, second_parts, third_parts))
    preceding = entering(signature, WIDE, combine, empty_state)
    result = combine(preceding, signature)
    return (
        path_points,
        result[0][None],
        result[1].reshape(1, path_width * path_width),
        result[2][None],
    )


def solution(mesh):
    finer = Mesh(mesh.devices.reshape(4, 4, mesh.shape["narrow"]), ("wide_0", "wide_1", "narrow"))
    return jax.shard_map(
        per_device,
        mesh=finer,
        in_specs=(P(WIDE_NARROW, None), P(), P(), P()),
        out_specs=(P(WIDE_NARROW, None), P(WIDE, None), P(WIDE, None), P(WIDE, "narrow", None)),
        check_vma=False,
    )
```

profile of v0, /device:TPU:64, one launch (start us, length us, event | category | flops | bytes accessed | tf_op | source)
XLA Modules:
  0.0 207.2 jit_solution(2240476632826139290)
XLA Ops:
  1.4 1.9 collective-permute-start
  3.3 7.9 %collective-permute-start.1 = (bf16[7,512]{1,0:T(8,128)(2,1)S(1)}, bf16[7,512]{1,0:T(8,128)(2,1)S(1)}, u32[]{:S(2)}, u32[]{:S(2)}) collective-permute-start(bf16[7,512]{1,0:T(8,128)(2,1)S(1)} %get-tuple-element.308), channel_id=1, source_target_pairs={{1,0},{2,1},{3,2},{4,3},{5,4},{6,5},{7,6},{8,7},{9,8},{10,9},{11,1... | collective-permute-start | bytes 21512 | tf_op jit(solution)/shard_map/ppermute | solution.py:22
  12.5 5.2 %concatenate.15 = bf16[1038,512]{1,0:T(8,128)(2,1)S(1)} concatenate(bf16[7,512]{1,0:T(8,128)(2,1)S(1)} %collective-permute-done, bf16[1024,512]{1,0:T(8,128)(2,1)} %param.8, bf16[7,512]{1,0:T(8,128)(2,1)S(1)} %collective-permute-done.1), dimensions={0} | concatenate | bytes 2125824 | tf_op jit(solution)/shard_map/concatenate | solution.py:23
  17.7 1.9 fusion.12
  19.7 1.8 fusion.30
  21.4 1.8 fusion.17
  24.7 1.4 fusion.11
  26.8 2.1 fusion.33
  28.9 3.4 %convolution_convert_fusion = bf16[1024,64]{0,1:T(8,128)(2,1)S(1)} fusion(bf16[512,64]{0,1:T(8,128)(2,1)S(1)} %copy-done, f32[1024,512]{1,0:T(8,128)} %fusion.33, f32[1024,512]{1,0:T(8,128)S(1)} %fusion.25, bf16[1032,512]{1,0:T(8,128)(2,1)S(1)} %fusion.11, f32[512]{0:T(512)S(1)} %bitcast.365, pred[1024]{0:T(1024)(128)(4,1)S(1)} %fusion.89, ...), kind=kOutput, calls=%fused_computation.45 | convolution fusion | flops 609812480 | bytes 7015424 | tf_op jit(solution)/shard_map/dot_general | solution.py:153
  32.4 2.1 %collective-permute-start.2 = (bf16[1,64]{0,1:T(8,128)(2,1)S(1)}, bf16[1,64]{0,1:T(8,128)(2,1)S(1)}, u32[]{:S(2)}, u32[]{:S(2)}) collective-permute-start(bf16[1,64]{0,1:T(8,128)(2,1)S(1)} %slice.301), channel_id=1, source_target_pairs={{0,1},{1,2},{2,3},{3,4},{4,5},{5,6},{6,7},{7,8},{8,9},{9,10},{10,1... | collective-permute-start | bytes 392 | tf_op jit(solution)/shard_map/ppermute | solution.py:30
  34.5 7.2 %collective-permute-done.2 = bf16[1,64]{0,1:T(8,128)(2,1)S(1)} collective-permute-done((bf16[1,64]{0,1:T(8,128)(2,1)S(1)}, bf16[1,64]{0,1:T(8,128)(2,1)S(1)}, u32[]{:S(2)}, u32[]{:S(2)}) %collective-permute-start.2) | collective-permute-done | bytes 160 | tf_op jit(solution)/shard_map/ppermute | solution.py:30
  41.9 0.8 reshape.563
  42.7 74.7 %while.32 = (s32[]{:T(128)}, f32[64]{0:T(128)S(1)}, f32[64,64]{1,0:T(8,128)S(1)}, f32[64,4096]{1,0:T(8,128)}, f32[4,256,64]{1,0,2:T(4,128)}, /*index=5*/s32[]{:T(128)}, f32[]{:T(128)}, s32[]{:T(128)}) while((s32[]{:T(128)}, f32[64]{0:T(128)S(1)}, f32[64,64]{1,0:T(8,128)S(1)}, f32[64,4096]{1,0:T(8,128)}, f32[4,256,64]{1,0,2:T(4,128)}, ...), condition=%wide.region_3.4_spmd.clone, body=%wide.region_0.3_spmd.clone.sunk | while | flops 1641513216 | bytes 33087340 | solution.py:181
  42.7 1.0 constant_dynamic-slice_fusion.17
  45.0 1.2 broadcast_multiply_fusion.9
  46.2 4.2 %fusion.125 = f32[4096,64]{0,1:T(8,128)S(1)} fusion(f32[256,4096]{0,1:T(8,128)S(1)} %bitcast.335, f32[64]{0:T(128)S(1)} %slice_reduce_fusion.13, f32[64,2,128]{2,0,1:T(8,128)S(1)} %reduce-window.14, f32[64,2]{0,1:T(2,128)S(1)} %slice.544), kind=kOutput, calls=%fused_computation.22.clone.1 | convolution fusion | flops 805339136 | bytes 5309184 | tf_op jit(solution)/shard_map/while/body/eval_jaxpr/nm,nk->mk/dot_general | solution.py:104
  50.4 4.2 %convolution_add_fusion.9 = f32[4096,64]{0,1:T(8,128)S(1)} fusion(f32[4096,64]{0,1:T(8,128)S(1)} %fusion.125, f32[256,4096]{0,1:T(8,128)S(1)} %bitcast.334, f32[1,256,64]{1,0,2:T(1,128)S(1)} %constant_dynamic-slice_fusion.17), kind=kOutput, calls=%fused_computation.10.clone.1 | convolution fusion | flops 805568512 | bytes 6356992 | tf_op jit(solution)/shard_map/while/body/eval_jaxpr/nm,nk->mk/dot_general | solution.py:105
  56.6 1.6 mul.1061
  58.2 2.4 %fusion.126 = f32[64,4096]{1,0:T(8,128)} fusion(f32[64,4096]{1,0:T(8,128)S(1)} %reshape.631, f32[64,4096]{1,0:T(8,128)} %get-tuple-element.453, f32[64,4096]{1,0:T(8,128)} %mul.1061, f32[4096]{0:T(1024)S(1)} %mul.1063, pred[]{:T(512)S(6)} %compare.8), kind=kLoop, calls=%fused_computation.17.clone.1 | loop fusion | flops 1048576 | bytes 4210689 | tf_op jit(solution)/shard_map/while/body/eval_jaxpr/add | solution.py:110
  61.1 1.0 constant_dynamic-slice_fusion.17
  63.4 1.2 broadcast_multiply_fusion.9
  64.6 4.2 %fusion.125 = f32[4096,64]{0,1:T(8,128)S(1)} fusion(f32[256,4096]{0,1:T(8,128)S(1)} %bitcast.335, f32[64]{0:T(128)S(1)} %slice_reduce_fusion.13, f32[64,2,128]{2,0,1:T(8,128)S(1)} %reduce-window.14, f32[64,2]{0,1:T(2,128)S(1)} %slice.544), kind=kOutput, calls=%fused_computation.22.clone.1 | convolution fusion | flops 805339136 | bytes 5309184 | tf_op jit(solution)/shard_map/while/body/eval_jaxpr/nm,nk->mk/dot_general | solution.py:104
  68.8 4.2 %convolution_add_fusion.9 = f32[4096,64]{0,1:T(8,128)S(1)} fusion(f32[4096,64]{0,1:T(8,128)S(1)} %fusion.125, f32[256,4096]{0,1:T(8,128)S(1)} %bitcast.334, f32[1,256,64]{1,0,2:T(1,128)S(1)} %constant_dynamic-slice_fusion.17), kind=kOutput, calls=%fused_computation.10.clone.1 | convolution fusion | flops 805568512 | bytes 6356992 | tf_op jit(solution)/shard_map/while/body/eval_jaxpr/nm,nk->mk/dot_general | solution.py:105
  75.0 1.6 mul.1061
  76.6 2.7 %fusion.126 = f32[64,4096]{1,0:T(8,128)} fusion(f32[64,4096]{1,0:T(8,128)S(1)} %reshape.631, f32[64,4096]{1,0:T(8,128)} %get-tuple-element.453, f32[64,4096]{1,0:T(8,128)} %mul.1061, f32[4096]{0:T(1024)S(1)} %mul.1063, pred[]{:T(512)S(6)} %compare.8), kind=kLoop, calls=%fused_computation.17.clone.1 | loop fusion | flops 1048576 | bytes 4210689 | tf_op jit(solution)/shard_map/while/body/eval_jaxpr/add | solution.py:110
  79.8 1.0 constant_dynamic-slice_fusion.17
  82.1 1.2 broadcast_multiply_fusion.9
  83.3 4.2 %fusion.125 = f32[4096,64]{0,1:T(8,128)S(1)} fusion(f32[256,4096]{0,1:T(8,128)S(1)} %bitcast.335, f32[64]{0:T(128)S(1)} %slice_reduce_fusion.13, f32[64,2,128]{2,0,1:T(8,128)S(1)} %reduce-window.14, f32[64,2]{0,1:T(2,128)S(1)} %slice.544), kind=kOutput, calls=%fused_computation.22.clone.1 | convolution fusion | flops 805339136 | bytes 5309184 | tf_op jit(solution)/shard_map/while/body/eval_jaxpr/nm,nk->mk/dot_general | solution.py:104
  87.5 4.2 %convolution_add_fusion.9 = f32[4096,64]{0,1:T(8,128)S(1)} fusion(f32[4096,64]{0,1:T(8,128)S(1)} %fusion.125, f32[256,4096]{0,1:T(8,128)S(1)} %bitcast.334, f32[1,256,64]{1,0,2:T(1,128)S(1)} %constant_dynamic-slice_fusion.17), kind=kOutput, calls=%fused_computation.10.clone.1 | convolution fusion | flops 805568512 | bytes 6356992 | tf_op jit(solution)/shard_map/while/body/eval_jaxpr/nm,nk->mk/dot_general | solution.py:105
  93.7 1.6 mul.1061
  95.3 2.7 %fusion.126 = f32[64,4096]{1,0:T(8,128)} fusion(f32[64,4096]{1,0:T(8,128)S(1)} %reshape.631, f32[64,4096]{1,0:T(8,128)} %get-tuple-element.453, f32[64,4096]{1,0:T(8,128)} %mul.1061, f32[4096]{0:T(1024)S(1)} %mul.1063, pred[]{:T(512)S(6)} %compare.8), kind=kLoop, calls=%fused_computation.17.clone.1 | loop fusion | flops 1048576 | bytes 4210689 | tf_op jit(solution)/shard_map/while/body/eval_jaxpr/add | solution.py:110
  98.5 1.0 constant_dynamic-slice_fusion.17
  100.8 1.2 broadcast_multiply_fusion.9
  102.0 4.2 %fusion.125 = f32[4096,64]{0,1:T(8,128)S(1)} fusion(f32[256,4096]{0,1:T(8,128)S(1)} %bitcast.335, f32[64]{0:T(128)S(1)} %slice_reduce_fusion.13, f32[64,2,128]{2,0,1:T(8,128)S(1)} %reduce-window.14, f32[64,2]{0,1:T(2,128)S(1)} %slice.544), kind=kOutput, calls=%fused_computation.22.clone.1 | convolution fusion | flops 805339136 | bytes 5309184 | tf_op jit(solution)/shard_map/while/body/eval_jaxpr/nm,nk->mk/dot_general | solution.py:104
  106.2 4.2 %convolution_add_fusion.9 = f32[4096,64]{0,1:T(8,128)S(1)} fusion(f32[4096,64]{0,1:T(8,128)S(1)} %fusion.125, f32[256,4096]{0,1:T(8,128)S(1)} %bitcast.334, f32[1,256,64]{1,0,2:T(1,128)S(1)} %constant_dynamic-slice_fusion.17), kind=kOutput, calls=%fused_computation.10.clone.1 | convolution fusion | flops 805568512 | bytes 6356992 | tf_op jit(solution)/shard_map/while/body/eval_jaxpr/nm,nk->mk/dot_general | solution.py:105
  112.4 1.6 mul.1061
  114.0 2.7 %fusion.126 = f32[64,4096]{1,0:T(8,128)} fusion(f32[64,4096]{1,0:T(8,128)S(1)} %reshape.631, f32[64,4096]{1,0:T(8,128)} %get-tuple-element.453, f32[64,4096]{1,0:T(8,128)} %mul.1061, f32[4096]{0:T(1024)S(1)} %mul.1063, pred[]{:T(512)S(6)} %compare.8), kind=kLoop, calls=%fused_computation.17.clone.1 | loop fusion | flops 1048576 | bytes 4210689 | tf_op jit(solution)/shard_map/while/body/eval_jaxpr/add | solution.py:110
  117.4 1.3 convert_bitcast_fusion
  118.7 1.2 copy.77
  120.4 3.8 %reduce.36 = bf16[64,4096]{1,0:T(8,128)(2,1)S(1)} reduce(bf16[64,1,4096]{2,1,0:T(2,128)(2,1)S(1)} %bitcast.339, bf16[]{:T(256)} %broadcast.413), dimensions={1}, to_apply=%bitcast.282.reduce_sub_computation | reduce | bytes 1048578
  124.2 1.3 reshape.628
  125.5 3.5 %all-to-all-start = ((bf16[8,2,16384]{2,1,0:T(2,128)(2,1)}), bf16[8,2,16384]{2,1,0:T(2,128)(2,1)S(1)}, u32[]{:S(2)}, u32[]{:S(2)}) async-start(bf16[8,2,16384]{2,1,0:T(2,128)(2,1)} %reshape.628), calls=%async_computation | async-start | bytes 1048576 | tf_op jit(solution)/shard_map/all_to_all | solution.py:182
  129.2 16.1 %all_gather.15 = f32[8,64,65]{2,1,0:T(8,128)S(1)} all-gather(f32[1,64,65]{2,1,0:T(8,128)S(1)} %pad_maximum_fusion), channel_id=1, replica_groups=mesh['wide_0'=4,'wide_1'=4,'narrow'=8] {'narrow'}, dimensions={0}, use_global_device_ids=true | all-gather | bytes 149760 | tf_op jit(solution)/shard_map/all_gather | solution.py:36
  146.2 1.1 bitcast_convert_fusion
  147.9 5.5 %while.33 = (s32[]{:T(128)}, f32[64]{0:T(128)S(1)}, f32[64,64]{1,0:T(8,128)S(1)}, f32[8,4096]{1,0:T(8,128)S(1)}, f32[8,64]{1,0:T(8,128)S(1)}, /*index=5*/f32[8,6...) while((s32[]{:T(128)}, f32[64]{0:T(128)S(1)}, ...), condition=%wide.region_5.6_spmd.clone, body=%wide.region_4.5_spmd.clone.sunk | while | flops 213123 | bytes 1122533 | solution.py:196
  153.6 15.3 %all-gather.2 = f32[4,10,4096]{2,1,0:T(8,128)S(1)} all-gather(f32[1,10,4096]{2,1,0:T(8,128)S(1)} %maximum_bitcast_fusion), channel_id=2, replica_groups=mesh['wide_0'=4,'wide_1'=4,'narrow'=8] {'wide_1'}, dimensions={0}, use_global_device_ids=true | all-gather | bytes 819200 | tf_op jit(solution)/shard_map/all_gather | solution.py:58
  173.4 14.0 %all-gather.3 = f32[4,10,4096]{2,1,0:T(8,128)S(1)} all-gather(f32[1,10,4096]{2,1,0:T(8,128)S(1)} %maximum_bitcast_fusion.1), channel_id=3, replica_groups=mesh['wide_0'=4,'wide_1'=4,'narrow'=8] {'wide_0'}, dimensions={0}, use_global_device_ids=true | all-gather | bytes 819200 | tf_op jit(solution)/shard_map/all_gather | solution.py:58
  205.3 1.9 fusion.65
  (298 shorter events, 48.6 us)
Async XLA Ops:
  0.6 28.2 %copy-start = (bf16[512,64]{0,1:T(8,128)(2,1)S(1)}, bf16[512,64]{0,1:T(8,128)(2,1)}, u32[]{:S(2)}) copy-start(bf16[512,64]{0,1:T(8,128)(2,1)} %param.11) | copy-start | bytes 196612
  1.4 10.7 %collective-permute-start = (bf16[7,512]{1,0:T(8,128)(2,1)S(1)}, bf16[7,512]{1,0:T(8,128)(2,1)S(1)}, u32[]{:S(2)}, u32[]{:S(2)}) collective-permute-start(bf16[7,512]{1,0:T(8,128)(2,1)S(1)} %get-tuple-element.309), channel_id=1, source_target_pairs={{0,1},{1,2},{2,3},{3,4},{4,5},{5,6},{6,7},{7,8},{8,9},{9,10},{10,1... | collective-permute-start | bytes 21512 | tf_op jit(solution)/shard_map/ppermute | solution.py:21
  3.3 9.2 %collective-permute-start.1 = (bf16[7,512]{1,0:T(8,128)(2,1)S(1)}, bf16[7,512]{1,0:T(8,128)(2,1)S(1)}, u32[]{:S(2)}, u32[]{:S(2)}) collective-permute-start(bf16[7,512]{1,0:T(8,128)(2,1)S(1)} %get-tuple-element.308), channel_id=1, source_target_pairs={{1,0},{2,1},{3,2},{4,3},{5,4},{6,5},{7,6},{8,7},{9,8},{10,9},{11,1... | collective-permute-start | bytes 21512 | tf_op jit(solution)/shard_map/ppermute | solution.py:22
  17.7 3.7 %copy-start.1 = (bf16[3,3,512,512]{3,2,1,0:T(8,128)(2,1)S(1)}, bf16[3,3,512,512]{3,2,1,0:T(8,128)(2,1)}, u32[]{:S(2)}) copy-start(bf16[3,3,512,512]{3,2,1,0:T(8,128)(2,1)} %param.9) | copy-start | bytes 14155780
  32.3 10.5 %copy-start.2 = (bf16[1024,64]{0,1:T(8,128)(2,1)}, bf16[1024,64]{0,1:T(8,128)(2,1)S(1)}, u32[]{:S(2)}) copy-start(bf16[1024,64]{0,1:T(8,128)(2,1)S(1)} %convolution_convert_fusion) | copy-start | bytes 393220
  32.4 9.3 %collective-permute-start.2 = (bf16[1,64]{0,1:T(8,128)(2,1)S(1)}, bf16[1,64]{0,1:T(8,128)(2,1)S(1)}, u32[]{:S(2)}, u32[]{:S(2)}) collective-permute-start(bf16[1,64]{0,1:T(8,128)(2,1)S(1)} %slice.301), channel_id=1, source_target_pairs={{0,1},{1,2},{2,3},{3,4},{4,5},{5,6},{6,7},{7,8},{8,9},{9,10},{10,1... | collective-permute-start | bytes 392 | tf_op jit(solution)/shard_map/ppermute | solution.py:30
  125.5 20.1 %all-to-all-start = ((bf16[8,2,16384]{2,1,0:T(2,128)(2,1)}), bf16[8,2,16384]{2,1,0:T(2,128)(2,1)S(1)}, u32[]{:S(2)}, u32[]{:S(2)}) async-start(bf16[8,2,16384]{2,1,0:T(2,128)(2,1)} %reshape.628), calls=%async_computation | async-start | bytes 1048576 | tf_op jit(solution)/shard_map/all_to_all | solution.py:182
  153.4 40.7 %copy-start.4 = (f32[64]{0:T(128)}, f32[64]{0:T(128)S(1)}, u32[]{:S(2)}) copy-start(f32[64]{0:T(128)S(1)} %get-tuple-element.136) | copy-start | bytes 772
  169.0 21.7 %copy-start.5 = (f32[64]{0:T(128)}, f32[64]{0:T(128)S(1)}, u32[]{:S(2)}) copy-start(f32[64]{0:T(128)S(1)} %get-tuple-element.273) | copy-start | bytes 772
  170.0 3.4 %copy-start.9 = (f32[8]{0:T(128)}, f32[8]{0:T(128)S(1)}, u32[]{:S(2)}) copy-start(f32[8]{0:T(128)S(1)} %dynamic_slice.88) | copy-start | bytes 100
  188.8 6.1 %copy-start.6 = (f32[64]{0:T(128)}, f32[64]{0:T(128)S(1)}, u32[]{:S(2)}) copy-start(f32[64]{0:T(128)S(1)} %get-tuple-element.312) | copy-start | bytes 772
  188.8 6.1 %copy-start.7 = (f32[64]{0:T(128)}, f32[64]{0:T(128)S(1)}, u32[]{:S(2)}) copy-start(f32[64]{0:T(128)S(1)} %get-tuple-element.313) | copy-start | bytes 772
  188.8 6.1 %copy-start.8 = (f32[64]{0:T(128)}, f32[64]{0:T(128)S(1)}, u32[]{:S(2)}) copy-start(f32[64]{0:T(128)S(1)} %get-tuple-element.314) | copy-start | bytes 772
  195.0 8.9 %copy-start.3 = (f32[64,64]{1,0:T(8,128)S(1)}, f32[64,64]{1,0:T(8,128)}, u32[]{:S(2)}) copy-start(f32[64,64]{1,0:T(8,128)} %get-tuple-element.265) | copy-start | bytes 49156
where the time goes:
time: 211 us; the launch traced here: 207 us
  local copies, waits for them, and re-layouts  52.4 us (25%)
  matrix products  49.9 us (24%)
  blocking collectives  45.4 us (22%)
  other arithmetic  34.4 us (16%)
  starting transfers between devices  15.4 us (7%)
  waiting for transfers between devices  7.61 us (4%)
    all_gather x2, blocking collectives, all_in_one(): both, at, found = (lax.all_gather(jnp.concatenate(lines), axis), 0, {})  29.3 us
    dot_general x4, matrix products, sig_update(): jnp.einsum('nm,nk->mk', third_terms, increments, precision=PRECISE)  16.8 us
    dot_general x4, matrix products, sig_update(): gained = jnp.einsum('nm,nk->mk', second_terms, remaining, precision=PRECISE)  16.7 us
    all_gather x1, blocking collectives, in_one_piece(): lax.all_gather(both, axis, axis=dim, tiled=True)  16.1 us
    dot_general x8, matrix products, apply_taps(): jnp.dot(window, weights[tap_idx], preferred_element_type=jnp.float32)  11.1 us
    add x4, other arithmetic, sig_update(): third_level + carried + gained.reshape(row_count, path_width * path_width)  10.5 us
    mul x16, local copies, waits for them, and re-layouts, sig_update(): second_rows[:, :, None] * totals[None, None, :]  9.31 us
    mul x56, local copies, waits for them, and re-layouts, chen(): second_rows[:, :, None] * first_b[None, None, :]  7.99 us
  transfers between devices with their start and end apart: 4, of which 2 were waited for; matrix products, arithmetic and copies ran while one was open for 1% of the time, Pallas kernels for 0%

commit v1 on v0

v1 whole, which is shorter than its diff:
```python
import functools

import jax
import jax.numpy as jnp
from jax import lax
from jax.experimental import pallas as pl
from jax.experimental.pallas import tpu as pltpu
from jax.sharding import PartitionSpec as P

C = 512
PATH = 64
TD = 1024
OFF = 32
ROWS = OFF + TD + 32
NX = 4
NZ = 4
NY = 4
TILE = 256
PAY = 256 + 64 + 16
MESH = pl.DeviceIdType.MESH
BF = jnp.bfloat16
F32 = jnp.float32


def silu(v):
    half = 0.5 * v
    return half + half * jnp.tanh(half)


def nt_dot(a, b):
    return lax.dot_general(a, b, (((1,), (1,)), ((), ())), preferred_element_type=F32)


def kernel(
    total_steps,
    rec_hbm,
    weight_hbm,
    bias_ref,
    proj_ref,
    path_ref,
    third_ref,
    second_ref,
    first_ref,
    weights,
    h0,
    h1,
    h2,
    seg,
    mid,
    step,
    centre,
    acc,
    level2,
    mine,
    partner_out,
    partner_in,
    out_x,
    in_x,
    out_z,
    in_z,
    w_sem,
    r_sem,
    halo_send,
    halo_recv,
    y_send,
    y_recv,
    p_send,
    p_recv,
    x_send,
    x_recv,
    z_send,
    z_recv,
):
    w = lax.axis_index("wide")
    n = lax.axis_index("narrow")
    z, x = lax.div(w, NX), lax.rem(w, NX)
    y, core = lax.div(n, 2), lax.rem(n, 2)
    g = w * 8 + n
    last_g = NX * NZ * 8 - 1
    has_left = g > 0
    has_right = g < last_g
    left = (lax.div(g + last_g, 8) % (NX * NZ), lax.rem(g + last_g, 8))
    right = (lax.div(g + 1, 8) % (NX * NZ), lax.rem(g + 1, 8))

    def y_peer(by):
        return (w, lax.rem(y + by, NY) * 2 + core)

    def x_peer(by):
        return (z * NX + lax.rem(x + by, NX), n)

    def z_peer(by):
        return ((z + by) * NX + x, n)

    partner = (w, y * 2 + 1 - core)

    weight_copies = [
        pltpu.make_async_copy(weight_hbm.at[l], weights.at[l], w_sem.at[l]) for l in range(3)
    ]
    own_copy = pltpu.make_async_copy(rec_hbm, h0.at[pl.ds(OFF, TD)], r_sem)
    own_copy.start()
    for copy in weight_copies:
        copy.start()

    barrier = pltpu.get_barrier_semaphore()

    @pl.when(has_left)
    def _():
        pl.semaphore_signal(barrier, inc=1, device_id=left, device_id_type=MESH)

    @pl.when(has_right)
    def _():
        pl.semaphore_signal(barrier, inc=1, device_id=right, device_id_type=MESH)

    for by in range(1, 4):
        pl.semaphore_signal(barrier, inc=1, device_id=y_peer(by), device_id_type=MESH)
        pl.semaphore_signal(barrier, inc=1, device_id=x_peer(by), device_id_type=MESH)

        @pl.when(z >= by)
        def _():
            pl.semaphore_signal(barrier, inc=1, device_id=z_peer(-by), device_id_type=MESH)

    pl.semaphore_signal(barrier, inc=1, device_id=partner, device_id_type=MESH)
    copied_to = has_left.astype(jnp.int32) + has_right.astype(jnp.int32) + 7 + (NZ - 1 - z)
    pl.semaphore_wait(barrier, copied_to)

    def remote(src, dst, send, recv, device):
        return pltpu.make_async_remote_copy(
            src_ref=src,
            dst_ref=dst,
            send_sem=send,
            recv_sem=recv,
            device_id=device,
            device_id_type=MESH,
        )

    to_left = remote(
        rec_hbm.at[pl.ds(0, 16)],
        h0.at[pl.ds(OFF + TD, 16)],
        halo_send.at[0],
        halo_recv.at[0],
        left,
    )
    to_right = remote(
        rec_hbm.at[pl.ds(TD - 16, 16)],
        h0.at[pl.ds(OFF - 16, 16)],
        halo_send.at[1],
        halo_recv.at[1],
        right,
    )

    @pl.when(has_left)
    def _():
        to_left.start()

    @pl.when(has_right)
    def _():
        to_right.start()

    def conv(layer, src, begin, end):
        d = 2**layer
        xs = [src[pl.ds(begin + (k - 1) * d, end - begin), :] for k in range(3)]
        centre_rows = xs[1].astype(F32)
        both = jnp.concatenate(xs, axis=1)
        totals = jnp.dot(both, weights[layer], preferred_element_type=F32)
        return (centre_rows + silu(totals + bias_ref[pl.ds(layer, 1), :])).astype(BF)

    first_tile, last_tile = (OFF - 16, OFF + 128), (OFF + TD - 128, OFF + TD + 16)
    tiles = [first_tile] + [(OFF + 128 * i, OFF + 128 * i + 128) for i in range(1, 7)] + [last_tile]

    def put(dst, rows, i):
        begin, end = tiles[i]
        dst[pl.ds(begin, end - begin), :] = rows
        if i == 0:
            dst[pl.ds(OFF - 16, 16), :] = jnp.where(has_left, rows[:16], jnp.zeros_like(rows[:16]))
        if i == 7:
            dst[pl.ds(OFF + TD, 16), :] = jnp.where(
                has_right, rows[128:], jnp.zeros_like(rows[128:])
            )

    own_copy.wait()
    weight_copies[0].wait()
    for i in range(1, 7):
        put(h1, conv(0, h0, *tiles[i]), i)

    @pl.when(has_left)
    def _():
        to_right.wait_recv()

    @pl.when(jnp.logical_not(has_left))
    def _():
        h0[pl.ds(OFF - 16, 16), :] = jnp.zeros((16, C), BF)

    @pl.when(has_right)
    def _():
        to_left.wait_recv()

    @pl.when(jnp.logical_not(has_right))
    def _():
        h0[pl.ds(OFF + TD, 16), :] = jnp.zeros((16, C), BF)

    put(h1, conv(0, h0, *tiles[7]), 7)
    put(h1, conv(0, h0, *tiles[0]), 0)

    y_copies = []

    def send_tile(t):
        lanes = pl.ds(0, 384) if t == 0 else pl.ds(128 + TILE * t, TILE)
        for slot, by in ((1, 1), (2, 3), (3, 2)):
            copy = remote(
                seg.at[0, :, lanes],
                seg.at[slot, :, lanes],
                y_send.at[slot - 1, t],
                y_recv.at[slot - 1, t],
                y_peer(by),
            )
            copy.start()
            y_copies.append(copy)

    def finish(i):
        begin, end = tiles[i]
        end = min(end, OFF + TD)
        rows = conv(2, h2, begin, end)
        points = jnp.dot(rows, proj_ref[...], preferred_element_type=F32).astype(BF)
        if i == 0:
            edge = points[:16].astype(F32)
            edge = jnp.where(has_left, edge, jnp.zeros_like(edge))
            edge = jnp.concatenate([jnp.zeros((112, PATH), F32), edge], axis=0)
            seg[0, :, pl.ds(0, 128)] = edge.T.astype(BF)
            points = points[16:]
        path_ref[pl.ds(128 * i, 128), :] = points
        seg[0, :, pl.ds(128 + 128 * i, 128)] = points.astype(F32).T.astype(BF)
        if i % 2 == 1:
            send_tile(i // 2)

    weight_copies[1].wait()
    put(h2, conv(1, h1, *tiles[0]), 0)
    put(h2, conv(1, h1, *tiles[1]), 1)
    weight_copies[2].wait()
    finish(0)
    for i in range(2, 8):
        put(h2, conv(1, h1, *tiles[i]), i)
        finish(i - 1)
    finish(7)

    own_points = seg[0, :, pl.ds(128, TD)].astype(F32)
    mean = jnp.sum(own_points, axis=1, keepdims=True) * (1.0 / TD)
    centre[...] = jnp.broadcast_to(mean, (PATH, 128))

    def prepare(slot, t):
        window = seg[slot, :, pl.ds(pl.multiple_of(TILE * t, TILE), 384)].astype(F32)
        now, before = window[:, 128:], window[:, 127:383]
        step[...] = now - before
        wide_centre = jnp.concatenate([centre[...]] * 2, axis=1)
        mid[...] = 0.5 * (now + before) - wide_centre

    def step_columns():
        d = step[...]
        high = d.astype(BF)
        low = (d - high.astype(F32)).astype(BF)
        return jnp.concatenate([high, low], axis=0)

    def add_rows(at, row_begin, columns):
        m = mid[...]
        d = step[...] * (1.0 / 12.0)
        rows = []
        for r in range(8):
            m_row = mid[pl.ds(row_begin + r, 1), :]
            d_row = step[pl.ds(row_begin + r, 1), :]
            rows.append((m_row * m + d_row * d).astype(BF))
        acc[pl.ds(at, 512), :] += nt_dot(jnp.concatenate(rows, axis=0), columns)

    def add_level2(columns):
        m = mid[...]
        high = m.astype(BF)
        low = (m - high.astype(F32)).astype(BF)
        ones = jnp.ones((16, TILE), BF)
        acc[pl.ds(1024, 144), :] += nt_dot(jnp.concatenate([high, low, ones], axis=0), columns)

    their_rows = y * 16 + (1 - core) * 8
    my_rows = y * 16 + core * 8
    acc[...] = jnp.zeros_like(acc)

    def wait_tile(slot, t):
        lanes = pl.ds(0, 384) if t == 0 else pl.ds(128 + TILE * t, TILE)
        remote(
            seg.at[0, :, lanes],
            seg.at[slot, :, lanes],
            y_send.at[slot - 1, t],
            y_recv.at[slot - 1, t],
            y_peer(1),
        ).wait_recv()

    def everything(slot, t):
        prepare(slot, t)
        columns = step_columns()
        add_rows(0, their_rows, columns)
        add_level2(columns)
        add_rows(512, my_rows, columns)

    def own_step(t, carry):
        everything(0, t)
        return carry

    lax.fori_loop(0, 4, own_step, 0)
    for t in range(3):
        for slot in range(1, 4):
            wait_tile(slot, t)

        def slot_step(slot, carry, t=t):
            everything(slot, t)
            return carry

        lax.fori_loop(1, 4, slot_step, 0)

    for slot in range(1, 4):
        wait_tile(slot, 3)

    def their_step(slot, carry):
        prepare(slot, 3)
        columns = step_columns()
        add_rows(0, their_rows, columns)
        add_level2(columns)
        return carry

    lax.fori_loop(1, 4, their_step, 0)

    lane = lax.broadcasted_iota(jnp.int32, (32, 128), 1)
    low_half = lane < 64

    def both_halves(v):
        return v + pltpu.roll(v, 64, 1)

    def packed(v):
        return jnp.where(low_half, v[:32], v[32:])

    local2 = both_halves(acc[pl.ds(1024, 64), :] + acc[pl.ds(1088, 64), :])
    delta = both_halves(acc[pl.ds(1152, 8), :])
    middle = centre[...]
    own2 = local2 + middle * delta[:1]
    level2[pl.ds(0, 64), :] = own2

    def third_rows(at, row_begin, dst):
        for r in range(8):
            block = both_halves(acc[pl.ds(at + 64 * r, 64), :])
            c_row = centre[pl.ds(row_begin + r, 1), :]
            s_row = level2[pl.ds(row_begin + r, 1), :]
            dst[pl.ds(32 * r, 32), :] = packed(block + c_row * local2 + middle * s_row)

    third_rows(0, their_rows, partner_out)
    partner_out[pl.ds(256, 32), :] = packed(own2)
    partner_out[pl.ds(288, 8), :] = delta
    swap = remote(partner_out, partner_in, p_send, p_recv, partner)
    swap.start()

    def my_step(slot, carry):
        prepare(slot, 3)
        add_rows(512, my_rows, step_columns())
        return carry

    lax.fori_loop(1, 4, my_step, 0)
    third_rows(512, my_rows, mine)
    mine[pl.ds(256, 32), :] = packed(own2)
    mine[pl.ds(288, 8), :] = delta
    swap.wait_recv()
    mine[...] += partner_in[...]

    def pack(dst, src):
        dst[pl.ds(0, 256), :] = src[pl.ds(0, 256), :].astype(BF)
        exact = src[pl.ds(256, 32), :]
        high = exact.astype(BF)
        dst[pl.ds(256, 32), :] = high
        dst[pl.ds(288, 32), :] = (exact - high.astype(F32)).astype(BF)
        exact = src[pl.ds(288, 8), :]
        high = exact.astype(BF).astype(F32)
        dst[pl.ds(320, 16), :] = jnp.concatenate([high, exact - high], axis=0).astype(BF)

    def unpack(src):
        third = src[pl.ds(0, 256), :].astype(F32)
        second = src[pl.ds(256, 32), :].astype(F32) + src[pl.ds(288, 32), :].astype(F32)
        pair = src[pl.ds(320, 16), :].astype(F32)
        return jnp.concatenate([third, second, pair[:8] + pair[8:]], axis=0)

    pack(out_x, mine)
    x_copies = []
    for by in range(1, 4):
        copy = remote(out_x, in_x.at[by - 1], x_send.at[by - 1], x_recv.at[by - 1], x_peer(by))
        copy.start()
        x_copies.append(copy)
    for copy in x_copies:
        copy.wait_recv()
    swap.wait_send()
    total = mine[...]
    upto = mine[...]
    for by in range(1, 4):
        other = unpack(in_x.at[by - 1])
        total = total + other
        upto = upto + jnp.where(x >= by, other, jnp.zeros_like(other))
    partner_out[...] = total
    mine[...] = upto
    pack(out_z, partner_out)
    z_copies = []
    for by in range(1, 4):
        z_copies.append(
            remote(out_z, in_z.at[by - 1], z_send.at[by - 1], z_recv.at[by - 1], z_peer(by))
        )

    for by in range(1, 4):

        @pl.when(z + by < NZ)
        def _():
            z_copies[by - 1].start()

    for by in range(1, 4):

        @pl.when(z >= by)
        def _():
            z_copies[by - 1].wait_recv()
            mine[...] += unpack(in_z.at[by - 1])

    scale = total_steps ** (-0.2)
    ends = mine[pl.ds(288, 8), :]
    columns = ends.T
    ends_k = jnp.where(
        low_half,
        jnp.broadcast_to(columns[:32, :1], (32, 128)),
        jnp.broadcast_to(columns[32:64, :1], (32, 128)),
    )
    first_ref[...] = ends * scale
    second_ref[...] = mine[pl.ds(256, 32), :] * scale**2
    in_high = n >= 4
    row_of = lax.rem(n, 4) * 8
    for r in range(8):
        row = mine[pl.ds(256 + row_of + r, 1), :]
        turned = pltpu.roll(row, 64, 1)
        low = lane[:1] < 64
        row = jnp.where(jnp.logical_xor(low, in_high), row, turned)
        third_ref[pl.ds(32 * r, 32), :] = (
            row * ends_k - mine[pl.ds(32 * r, 32), :]
        ) * scale**3

    @pl.when(has_left)
    def _():
        to_left.wait_send()

    @pl.when(has_right)
    def _():
        to_right.wait_send()

    for copy in y_copies + x_copies:
        copy.wait_send()
    for by in range(1, 4):

        @pl.when(z + by < NZ)
        def _():
            z_copies[by - 1].wait_send()


def per_device(total_steps, recording, conv_weight, conv_bias, projection):
    vmem = pl.BlockSpec(memory_space=pltpu.VMEM)
    anywhere = pl.BlockSpec(memory_space=pl.ANY)
    path_points, third, second, first = pl.pallas_call(
        functools.partial(kernel, total_steps),
        out_shape=(
            jax.ShapeDtypeStruct((TD, PATH), BF),
            jax.ShapeDtypeStruct((256, 128), F32),
            jax.ShapeDtypeStruct((32, 128), F32),
            jax.ShapeDtypeStruct((8, 128), F32),
        ),
        in_specs=[anywhere, anywhere, vmem, vmem],
        out_specs=(vmem, vmem, vmem, vmem),
        scratch_shapes=[
            pltpu.VMEM((3, 3 * C, C), BF),
            pltpu.VMEM((ROWS, C), BF),
            pltpu.VMEM((ROWS, C), BF),
            pltpu.VMEM((ROWS, C), BF),
            pltpu.VMEM((4, PATH, 128 + TD), BF),
            pltpu.VMEM((PATH, TILE), F32),
            pltpu.VMEM((PATH, TILE), F32),
            pltpu.VMEM((PATH, 128), F32),
            pltpu.VMEM((1168, 128), F32),
            pltpu.VMEM((64, 128), F32),
            pltpu.VMEM((296, 128), F32),
            pltpu.VMEM((296, 128), F32),
            pltpu.VMEM((296, 128), F32),
            pltpu.VMEM((PAY, 128), BF),
            pltpu.VMEM((3, PAY, 128), BF),
            pltpu.VMEM((PAY, 128), BF),
            pltpu.VMEM((3, PAY, 128), BF),
            pltpu.SemaphoreType.DMA((3,)),
            pltpu.SemaphoreType.DMA,
            pltpu.SemaphoreType.DMA((2,)),
            pltpu.SemaphoreType.DMA((2,)),
            pltpu.SemaphoreType.DMA((3, 4)),
            pltpu.SemaphoreType.DMA((3, 4)),
            pltpu.SemaphoreType.DMA,
            pltpu.SemaphoreType.DMA,
            pltpu.SemaphoreType.DMA((3,)),
            pltpu.SemaphoreType.DMA((3,)),
            pltpu.SemaphoreType.DMA((3,)),
            pltpu.SemaphoreType.DMA((3,)),
        ],
        compiler_params=pltpu.CompilerParams(
            collective_id=0, has_side_effects=True, vmem_limit_bytes=48 << 20
        ),
    )(recording, conv_weight.reshape(3, 3 * C, C), conv_bias, projection)
    second = second.reshape(32, 2, PATH).transpose(1, 0, 2).reshape(1, PATH * PATH)
    third = third.reshape(8, 32, 2, PATH).transpose(0, 3, 2, 1).reshape(1, 8, PATH * PATH)
    return path_points, first[:1, :PATH], second, third


def solution(mesh):
    total_steps = TD * mesh.shape["wide"] * mesh.shape["narrow"]
    return jax.shard_map(
        functools.partial(per_device, total_steps),
        mesh=mesh,
        in_specs=(P(("wide", "narrow"), None), P(), P(), P()),
        out_specs=(
            P(("wide", "narrow"), None),
            P("wide", None),
            P("wide", None),
            P("wide", "narrow", None),
        ),
        check_vma=False,
    )
```

time: 211 us -> 43.1 us (0.20); the launches traced: 207 us -> 42.6 us
  matrix products: 49.9 us -> 0 us
  local copies, waits for them, and re-layouts: 52.4 us -> 6.73 us
  blocking collectives: 45.4 us -> 0 us
  Pallas kernels: 0 us -> 35.2 us
  other arithmetic: 34.4 us -> 0 us
  starting transfers between devices: 15.4 us -> 0 us
  waiting for transfers between devices: 7.61 us -> 0 us
    dot_general x25 -> x0, matrix products: 49.9 us -> none  [the longest x4 16.8 us: sig_update(): jnp.einsum('nm,nk->mk', third_terms, increments, precision=PRECISE)]
    all_gather x3 -> x0, blocking collectives: 45.4 us -> none  [the longest x2 29.3 us: all_in_one(): both, at, found = (lax.all_gather(jnp.concatenate(lines), axis), 0, {})]
    pallas_call x0 -> x1, Pallas kernels: none -> 35.2 us  [per_device(): pl.pallas_call(functools.partial(kernel, total_steps), out_shape=(jax.Sha...]
    mul x108 -> x0, local copies, waits for them, and re-layouts: 22.8 us -> none  [the longest x16 9.31 us: sig_update(): second_rows[:, :, None] * totals[None, None, :]]
    add x44 -> x0, other arithmetic: 15.5 us -> none  [the longest x4 10.5 us: sig_update(): third_level + carried + gained.reshape(row_count, path_width * path_width)]
    ppermute x3 -> x0, starting transfers between devices: 11.9 us -> none  [the longest x1 7.86 us: padded_2(): after = lax.ppermute(first, axis, down)]
    dynamic_slice x35 -> x0, local copies, waits for them, and re-layouts: 7.9 us -> none  [the longest x8 4.07 us: per_device(): partial_sig, unused = lax.scan(whole_step, whole_empty, quarters)]
    ppermute x3 -> x0, waiting for transfers between devices: 7.61 us -> none  [the longest x1 7.17 us: from_behind(): return lax.ppermute(array, axis, pairs)]
  transfers between devices with their start and end apart: 4 -> 0, of which waited for: 2 -> 0; matrix products, arithmetic and copies ran while one was open for 1% -> 0% of each run, Pallas kernels for 0% -> 0%
where the time goes in v1:
time: 43.1 us; the launch traced here: 42.6 us
  Pallas kernels  35.2 us (82%)
  local copies, waits for them, and re-layouts  6.73 us (16%)
  between operations  0.68 us (2%)
    pallas_call x1, Pallas kernels, per_device(): pl.pallas_call(functools.partial(kernel, total_steps), out_shape=(jax.Sha...  35.2 us
    unnamed x6, local copies, waits for them, and re-layouts  3.66 us
    reshape x3, local copies, waits for them, and re-layouts, per_device(): third.reshape(8, 32, 2, PATH).transpose(0, 3, 2, 1)  1.78 us

profile of v1, /device:TPU:64, one launch (start us, length us, event | category | flops | bytes accessed | tf_op | source)
XLA Modules:
  0.0 42.6 jit_solution(18372013893537394852)
XLA Ops:
  0.6 1.0 %copy.12.proj_ref = bf16[512,64]{1,0:T(8,128)(2,1)S(1)} copy(bf16[512,64]{0,1:T(8,128)(2,1)} %param.7) | data formatting | bytes 131072 | tf_op args[3]
  1.6 0.0 copy-start
  1.6 1.2 %copy-done = bf16[1024,512]{1,0:T(8,128)(2,1)S(1)} copy-done((bf16[1024,512]{1,0:T(8,128)(2,1)S(1)}, bf16[1024,512]{1,0:T(8,128)(2,1)}, u32[]{:S(2)}) %copy-start) | copy-done | bytes 1048600
  2.8 0.0 copy-start.1
  2.8 0.7 %copy-done.1 = f32[3,512]{1,0:T(4,128)S(1)} copy-done((f32[3,512]{1,0:T(4,128)S(1)}, f32[3,512]{1,0:T(4,128)}, u32[]{:S(2)}) %copy-start.1) | copy-done | bytes 6168
  3.5 35.2 %shard_map.75 = (bf16[1024,64]{1,0:T(8,128)(2,1)S(1)}, f32[256,128]{1,0:T(8,128)S(1)}, f32[32,128]{1,0:T(8,128)S(1)}, f32[8,128]{1,0:T(8,128)S(1)}) custom-call(bf16[1024,512]{1,0:T(8,128)(2,1)S(1)} %copy-done, bf16[3,1536,512]{2,1,0:T(8,128)(2,1)} %bitcast.3, f32[3,512]{1,0:T(4,128)S(1)} %copy-done.1, bf16[512,64]{1,0:T(8,128)(2,1)S(1)} %copy.12.proj_ref), custom_call_target="tpu_custom_call" | custom-call | tf_op jit(solution)/shard_map/pallas_call | solution.py:461
  38.7 0.8 %copy.15 = bf16[1024,64]{0,1:T(8,128)(2,1)} copy(bf16[1024,64]{1,0:T(8,128)(2,1)S(1)} %get-tuple-element.16) | data formatting | bytes 262144
  39.5 0.5 %slice.3 = f32[1,64]{1,0:T(1,128)} slice(f32[8,128]{1,0:T(8,128)S(1)} %get-tuple-element.9), slice={[0:1], [0:64]} | slice | bytes 512 | tf_op jit(solution)/shard_map/slice | solution.py:508
  40.0 0.1 reshape.24
  40.1 0.7 %reshape.25 = f32[1,4096]{1,0:T(1,128)} reshape(f32[2,32,64]{2,1,0:T(8,128)S(1)} %copy.13) | data formatting | bytes 32768 | tf_op jit(solution)/shard_map/reshape | solution.py:506
  40.8 0.2 reshape.26
  41.0 0.3 copy.14
  41.3 1.3 %reshape.27 = f32[1,8,4096]{2,1,0:T(8,128)} reshape(f32[8,64,2,32]{3,2,1,0:T(2,128)S(1)} %bitcast.4) | data formatting | bytes 262144 | tf_op jit(solution)/shard_map/reshape | solution.py:507
  (1 shorter events, 0.0 us)
Async XLA Ops:
  1.6 1.2 %copy-start = (bf16[1024,512]{1,0:T(8,128)(2,1)S(1)}, bf16[1024,512]{1,0:T(8,128)(2,1)}, u32[]{:S(2)}) copy-start(bf16[1024,512]{1,0:T(8,128)(2,1)} %rec_hbm.1) | copy-start | bytes 3145732
  2.8 0.7 %copy-start.1 = (f32[3,512]{1,0:T(4,128)S(1)}, f32[3,512]{1,0:T(4,128)}, u32[]{:S(2)}) copy-start(f32[3,512]{1,0:T(4,128)} %bias_ref.1) | copy-start | bytes 18436

commit v2 on v1

--- a/solution.py
+++ b/solution.py
@@ -35,13 +35,15 @@
     total_steps,
     rec_hbm,
     weight_hbm,
-    bias_ref,
-    proj_ref,
+    bias_hbm,
+    proj_hbm,
     path_ref,
     third_ref,
     second_ref,
     first_ref,
     weights,
+    bias_ref,
+    proj_ref,
     h0,
     h1,
     h2,
@@ -52,6 +54,7 @@
     acc,
     level2,
     mine,
+    turned,
     partner_out,
     partner_in,
     out_x,
@@ -59,6 +62,7 @@
     out_z,
     in_z,
     w_sem,
+    small_sem,
     r_sem,
     halo_send,
     halo_recv,
@@ -97,9 +101,15 @@
         pltpu.make_async_copy(weight_hbm.at[l], weights.at[l], w_sem.at[l]) for l in range(3)
     ]
     own_copy = pltpu.make_async_copy(rec_hbm, h0.at[pl.ds(OFF, TD)], r_sem)
+    small_copies = [
+        pltpu.make_async_copy(bias_hbm, bias_ref, small_sem.at[0]),
+        pltpu.make_async_copy(proj_hbm, proj_ref, small_sem.at[1]),
+    ]
     own_copy.start()
+    small_copies[0].start()
     for copy in weight_copies:
         copy.start()
+    small_copies[1].start()
 
     barrier = pltpu.get_barrier_semaphore()
 
@@ -178,6 +188,7 @@
             )
 
     own_copy.wait()
+    small_copies[0].wait()
     weight_copies[0].wait()
     for i in range(1, 7):
         put(h1, conv(0, h0, *tiles[i]), i)
@@ -220,15 +231,14 @@
         begin, end = tiles[i]
         end = min(end, OFF + TD)
         rows = conv(2, h2, begin, end)
-        points = jnp.dot(rows, proj_ref[...], preferred_element_type=F32).astype(BF)
+        points = nt_dot(proj_ref[...], rows)
         if i == 0:
-            edge = points[:16].astype(F32)
-            edge = jnp.where(has_left, edge, jnp.zeros_like(edge))
-            edge = jnp.concatenate([jnp.zeros((112, PATH), F32), edge], axis=0)
-            seg[0, :, pl.ds(0, 128)] = edge.T.astype(BF)
-            points = points[16:]
-        path_ref[pl.ds(128 * i, 128), :] = points
-        seg[0, :, pl.ds(128 + 128 * i, 128)] = points.astype(F32).T.astype(BF)
+            edge = jnp.where(has_left, points[:, 15:16], jnp.zeros((PATH, 1), F32))
+            seg[0, :, pl.ds(0, 128)] = jnp.broadcast_to(edge, (PATH, 128)).astype(BF)
+            points = points[:, 16:]
+        points = points.astype(BF)
+        path_ref[:, pl.ds(128 * i, 128)] = points
+        seg[0, :, pl.ds(128 + 128 * i, 128)] = points
         if i % 2 == 1:
             send_tile(i // 2)
 
@@ -236,6 +246,7 @@
     put(h2, conv(1, h1, *tiles[0]), 0)
     put(h2, conv(1, h1, *tiles[1]), 1)
     weight_copies[2].wait()
+    small_copies[1].wait()
     finish(0)
     for i in range(2, 8):
         put(h2, conv(1, h1, *tiles[i]), i)
@@ -246,31 +257,31 @@
     mean = jnp.sum(own_points, axis=1, keepdims=True) * (1.0 / TD)
     centre[...] = jnp.broadcast_to(mean, (PATH, 128))
 
-    def prepare(slot, t):
-        window = seg[slot, :, pl.ds(pl.multiple_of(TILE * t, TILE), 384)].astype(F32)
+    def prepare(slot, t, buf):
+        window = seg[slot, :, pl.ds(TILE * t, 384)].astype(F32)
         now, before = window[:, 128:], window[:, 127:383]
-        step[...] = now - before
+        step[buf] = now - before
         wide_centre = jnp.concatenate([centre[...]] * 2, axis=1)
-        mid[...] = 0.5 * (now + before) - wide_centre
-
-    def step_columns():
-        d = step[...]
+        mid[buf] = 0.5 * (now + before) - wide_centre
+
+    def step_columns(buf):
+        d = step[buf]
         high = d.astype(BF)
         low = (d - high.astype(F32)).astype(BF)
         return jnp.concatenate([high, low], axis=0)
 
-    def add_rows(at, row_begin, columns):
-        m = mid[...]
-        d = step[...] * (1.0 / 12.0)
+    def add_rows(at, row_begin, buf, columns):
+        m = mid[buf]
+        d = step[buf] * (1.0 / 12.0)
         rows = []
         for r in range(8):
-            m_row = mid[pl.ds(row_begin + r, 1), :]
-            d_row = step[pl.ds(row_begin + r, 1), :]
+            m_row = mid[buf, pl.ds(row_begin + r, 1), :]
+            d_row = step[buf, pl.ds(row_begin + r, 1), :]
             rows.append((m_row * m + d_row * d).astype(BF))
         acc[pl.ds(at, 512), :] += nt_dot(jnp.concatenate(rows, axis=0), columns)
 
-    def add_level2(columns):
-        m = mid[...]
+    def add_level2(buf, columns):
+        m = mid[buf]
         high = m.astype(BF)
         low = (m - high.astype(F32)).astype(BF)
         ones = jnp.ones((16, TILE), BF)
@@ -290,48 +301,36 @@
             y_peer(1),
         ).wait_recv()
 
-    def everything(slot, t):
-        prepare(slot, t)
-        columns = step_columns()
-        add_rows(0, their_rows, columns)
-        add_level2(columns)
-        add_rows(512, my_rows, columns)
-
-    def own_step(t, carry):
-        everything(0, t)
-        return carry
-
-    lax.fori_loop(0, 4, own_step, 0)
-    for t in range(3):
-        for slot in range(1, 4):
-            wait_tile(slot, t)
-
-        def slot_step(slot, carry, t=t):
-            everything(slot, t)
-            return carry
-
-        lax.fori_loop(1, 4, slot_step, 0)
-
+    def everything(steps):
+        for at, (slot, t) in enumerate(steps):
+            prepare(slot, t, at % 4)
+            columns = step_columns(at % 4)
+            add_rows(0, their_rows, at % 4, columns)
+            add_level2(at % 4, columns)
+            add_rows(512, my_rows, at % 4, columns)
+
+    everything([(0, t) for t in range(4)])
+    for group in ((0, 1), (2,)):
+        for t in group:
+            for slot in range(1, 4):
+                wait_tile(slot, t)
+        everything([(slot, t) for t in group for slot in range(1, 4)])
     for slot in range(1, 4):
         wait_tile(slot, 3)
-
-    def their_step(slot, carry):
-        prepare(slot, 3)
-        columns = step_columns()
-        add_rows(0, their_rows, columns)
-        add_level2(columns)
-        return carry
-
-    lax.fori_loop(1, 4, their_step, 0)
-
-    lane = lax.broadcasted_iota(jnp.int32, (32, 128), 1)
-    low_half = lane < 64
+    for slot in range(1, 4):
+        prepare(slot, 3, slot)
+        columns = step_columns(slot)
+        add_rows(0, their_rows, slot, columns)
+        add_level2(slot, columns)
+
+    low_half = lax.broadcasted_iota(jnp.int32, (64, 128), 1) < 64
 
     def both_halves(v):
         return v + pltpu.roll(v, 64, 1)
 
-    def packed(v):
-        return jnp.where(low_half, v[:32], v[32:])
+    def packed_level2():
+        even, odd = level2[pl.ds(0, 32, stride=2), :], level2[pl.ds(1, 32, stride=2), :]
+        return jnp.where(low_half[:32], even, odd)
 
     local2 = both_halves(acc[pl.ds(1024, 64), :] + acc[pl.ds(1088, 64), :])
     delta = both_halves(acc[pl.ds(1152, 8), :])
@@ -340,26 +339,25 @@
     level2[pl.ds(0, 64), :] = own2
 
     def third_rows(at, row_begin, dst):
-        for r in range(8):
-            block = both_halves(acc[pl.ds(at + 64 * r, 64), :])
+        def block(r):
+            rows = both_halves(acc[pl.ds(at + 64 * r, 64), :])
             c_row = centre[pl.ds(row_begin + r, 1), :]
             s_row = level2[pl.ds(row_begin + r, 1), :]
-            dst[pl.ds(32 * r, 32), :] = packed(block + c_row * local2 + middle * s_row)
+            return rows + c_row * local2 + middle * s_row
+
+        for r in range(4):
+            dst[pl.ds(64 * r, 64), :] = jnp.where(low_half, block(r), block(r + 4))
 
     third_rows(0, their_rows, partner_out)
-    partner_out[pl.ds(256, 32), :] = packed(own2)
+    partner_out[pl.ds(256, 32), :] = packed_level2()
     partner_out[pl.ds(288, 8), :] = delta
     swap = remote(partner_out, partner_in, p_send, p_recv, partner)
     swap.start()
 
-    def my_step(slot, carry):
-        prepare(slot, 3)
-        add_rows(512, my_rows, step_columns())
-        return carry
-
-    lax.fori_loop(1, 4, my_step, 0)
+    for slot in range(1, 4):
+        add_rows(512, my_rows, slot, step_columns(slot))
     third_rows(512, my_rows, mine)
-    mine[pl.ds(256, 32), :] = packed(own2)
+    mine[pl.ds(256, 32), :] = packed_level2()
     mine[pl.ds(288, 8), :] = delta
     swap.wait_recv()
     mine[...] += partner_in[...]
@@ -419,24 +417,24 @@
 
     scale = total_steps ** (-0.2)
     ends = mine[pl.ds(288, 8), :]
-    columns = ends.T
-    ends_k = jnp.where(
-        low_half,
-        jnp.broadcast_to(columns[:32, :1], (32, 128)),
-        jnp.broadcast_to(columns[32:64, :1], (32, 128)),
-    )
-    first_ref[...] = ends * scale
+    ends_k = jnp.broadcast_to(ends.T[:64, :1], (64, 128))
+    first_ref[...] = ends[:1, :64] * scale
     second_ref[...] = mine[pl.ds(256, 32), :] * scale**2
-    in_high = n >= 4
-    row_of = lax.rem(n, 4) * 8
-    for r in range(8):
-        row = mine[pl.ds(256 + row_of + r, 1), :]
-        turned = pltpu.roll(row, 64, 1)
-        low = lane[:1] < 64
-        row = jnp.where(jnp.logical_xor(low, in_high), row, turned)
-        third_ref[pl.ds(32 * r, 32), :] = (
-            row * ends_k - mine[pl.ds(32 * r, 32), :]
-        ) * scale**3
+
+    def level2_row(r):
+        row = mine[pl.ds(256 + 4 * n + r // 2, 1), :]
+        other = pltpu.roll(row, 64, 1)
+        low = low_half[:1]
+        return jnp.where(low, row, other) if r % 2 == 0 else jnp.where(low, other, row)
+
+    for r in range(4):
+        row = jnp.where(low_half[:1], level2_row(r), level2_row(r + 4))
+        values = ((row * ends_k - mine[pl.ds(64 * r, 64), :]) * scale**3).T
+        turned[pl.ds(r, 64, stride=8), :] = values[:64]
+        turned[pl.ds(4 + r, 64, stride=8), :] = values[64:]
+    for pair in range(32):
+        both = [turned[pl.ds(16 * pair + 8 * k, 8), :] for k in range(2)]
+        third_ref[:, pl.ds(128 * pair, 128)] = jnp.concatenate(both, axis=1)
 
     @pl.when(has_left)
     def _():
@@ -457,29 +455,32 @@
 
 def per_device(total_steps, recording, conv_weight, conv_bias, projection):
     vmem = pl.BlockSpec(memory_space=pltpu.VMEM)
-    anywhere = pl.BlockSpec(memory_space=pl.ANY)
+    hbm = pl.BlockSpec(memory_space=pltpu.HBM)
     path_points, third, second, first = pl.pallas_call(
         functools.partial(kernel, total_steps),
         out_shape=(
-            jax.ShapeDtypeStruct((TD, PATH), BF),
-            jax.ShapeDtypeStruct((256, 128), F32),
+            jax.ShapeDtypeStruct((PATH, TD), BF),
+            jax.ShapeDtypeStruct((8, PATH * PATH), F32),
             jax.ShapeDtypeStruct((32, 128), F32),
-            jax.ShapeDtypeStruct((8, 128), F32),
+            jax.ShapeDtypeStruct((1, PATH), F32),
         ),
-        in_specs=[anywhere, anywhere, vmem, vmem],
+        in_specs=[hbm, hbm, hbm, hbm],
         out_specs=(vmem, vmem, vmem, vmem),
         scratch_shapes=[
             pltpu.VMEM((3, 3 * C, C), BF),
+            pltpu.VMEM((3, C), F32),
+            pltpu.VMEM((PATH, C), BF),
             pltpu.VMEM((ROWS, C), BF),
             pltpu.VMEM((ROWS, C), BF),
             pltpu.VMEM((ROWS, C), BF),
             pltpu.VMEM((4, PATH, 128 + TD), BF),
-            pltpu.VMEM((PATH, TILE), F32),
-            pltpu.VMEM((PATH, TILE), F32),
+            pltpu.VMEM((4, PATH, TILE), F32),
+            pltpu.VMEM((4, PATH, TILE), F32),
             pltpu.VMEM((PATH, 128), F32),
             pltpu.VMEM((1168, 128), F32),
             pltpu.VMEM((64, 128), F32),
             pltpu.VMEM((296, 128), F32),
+            pltpu.VMEM((512, PATH), F32),
             pltpu.VMEM((296, 128), F32),
             pltpu.VMEM((296, 128), F32),
             pltpu.VMEM((PAY, 128), BF),
@@ -487,6 +488,7 @@
             pltpu.VMEM((PAY, 128), BF),
             pltpu.VMEM((3, PAY, 128), BF),
             pltpu.SemaphoreType.DMA((3,)),
+            pltpu.SemaphoreType.DMA((2,)),
             pltpu.SemaphoreType.DMA,
             pltpu.SemaphoreType.DMA((2,)),
             pltpu.SemaphoreType.DMA((2,)),
@@ -500,12 +502,10 @@
             pltpu.SemaphoreType.DMA((3,)),
         ],
         compiler_params=pltpu.CompilerParams(
-            collective_id=0, has_side_effects=True, vmem_limit_bytes=48 << 20
+            collective_id=0, has_side_effects=True, vmem_limit_bytes=67043328
         ),
-    )(recording, conv_weight.reshape(3, 3 * C, C), conv_bias, projection)
-    second = second.reshape(32, 2, PATH).transpose(1, 0, 2).reshape(1, PATH * PATH)
-    third = third.reshape(8, 32, 2, PATH).transpose(0, 3, 2, 1).reshape(1, 8, PATH * PATH)
-    return path_points, first[:1, :PATH], second, third
+    )(recording, conv_weight.reshape(3, 3 * C, C), conv_bias, projection.T)
+    return path_points.T, first, second.reshape(1, PATH * PATH), third[None]
 
 
 def solution(mesh):

time: 43.1 us -> 40.4 us (0.937)
  Pallas kernels: 35.2 us -> 34 us
  local copies, waits for them, and re-layouts: 6.73 us -> 5.54 us
    reshape x5 -> x0, local copies, waits for them, and re-layouts: 2.55 us -> none  [the longest x3 1.78 us: per_device(): third.reshape(8, 32, 2, PATH).transpose(0, 3, 2, 1)]
    unnamed x6 -> x4, local copies, waits for them, and re-layouts: 3.66 us -> 5.54 us
    pallas_call x1, Pallas kernels: 35.2 us -> 34 us  [per_device(): pl.pallas_call(functools.partial(kernel, total_steps), out_shape=(jax.Sha...]
    slice x1 -> x0, local copies, waits for them, and re-layouts: 0.51 us -> none  [per_device(): return (path_points, first[:1, :PATH], second, third)]
where the time goes in v2:
time: 40.4 us; the launch traced here: 40.2 us
  Pallas kernels  34 us (84%)
  local copies, waits for them, and re-layouts  5.54 us (14%)
  between operations  0.64 us (2%)
    pallas_call x1, Pallas kernels, per_device(): pl.pallas_call(functools.partial(kernel, total_steps), out_shape=(jax.Sha...  34 us
    unnamed x4, local copies, waits for them, and re-layouts  5.54 us

profile of v2, /device:TPU:64, one launch (start us, length us, event | category | flops | bytes accessed | tf_op | source)
XLA Modules:
  0.0 40.2 jit_solution(17137008315384023538)
XLA Ops:
  0.6 34.0 %shard_map.75 = (bf16[64,1024]{1,0:T(8,128)(2,1)}, f32[8,4096]{1,0:T(8,128)}, f32[32,128]{1,0:T(8,128)}, f32[1,64]{1,0:T(1,128)}) custom-call(bf16[1024,512]{1,0:T(8,128)(2,1)} %rec_hbm.1, bf16[3,1536,512]{2,1,0:T(8,128)(2,1)} %bitcast.5, f32[3,512]{1,0:T(4,128)} %bias_hbm.1, bf16[64,512]{1,0:T(8,128)(2,1)} %bitcast.8), custom_call_target="tpu_custom_call" | custom-call | tf_op jit(solution)/shard_map/pallas_call | solution.py:459
  34.6 1.6 %copy.12 = bf16[1024,64]{0,1:T(8,128)(2,1)} copy(bf16[1024,64]{0,1:T(8,128)(2,1)} %bitcast.7) | data formatting | bytes 262144
  36.2 1.1 %copy.13 = f32[1,64]{1,0:T(1,128)} copy(f32[1,64]{1,0:T(1,128)} %get-tuple-element.17) | data formatting | bytes 512
  37.3 1.3 %copy.14 = f32[1,4096]{1,0:T(1,128)} copy(f32[1,4096]{1,0:T(1,128)} %bitcast.9) | data formatting | bytes 32768
  38.6 1.6 %copy.15 = f32[1,8,4096]{2,1,0:T(8,128)} copy(f32[1,8,4096]{2,1,0:T(8,128)} %bitcast.6) | data formatting | bytes 262144

commit v3 on v2

--- a/solution.py
+++ b/solution.py
@@ -456,6 +456,8 @@
 def per_device(total_steps, recording, conv_weight, conv_bias, projection):
     vmem = pl.BlockSpec(memory_space=pltpu.VMEM)
     hbm = pl.BlockSpec(memory_space=pltpu.HBM)
+    operands = (recording, conv_weight.reshape(3, 3 * C, C), conv_bias, projection.T)
+    operands = [pltpu.with_memory_space_constraint(a, pltpu.HBM) for a in operands]
     path_points, third, second, first = pl.pallas_call(
         functools.partial(kernel, total_steps),
         out_shape=(
@@ -502,9 +504,9 @@
             pltpu.SemaphoreType.DMA((3,)),
         ],
         compiler_params=pltpu.CompilerParams(
-            collective_id=0, has_side_effects=True, vmem_limit_bytes=67043328
+            collective_id=0, has_side_effects=True, vmem_limit_bytes=48 << 20
         ),
-    )(recording, conv_weight.reshape(3, 3 * C, C), conv_bias, projection.T)
+    )(*operands)
     return path_points.T, first, second.reshape(1, PATH * PATH), third[None]
 
 

time: 40.4 us -> 36.5 us (0.903)
  local copies, waits for them, and re-layouts: 5.54 us -> 2.43 us
  Pallas kernels: 34 us -> 33.3 us
    unnamed x4, local copies, waits for them, and re-layouts: 5.54 us -> 2.43 us
    pallas_call x1, Pallas kernels: 34 us -> 33.3 us  [per_device(): pl.pallas_call(functools.partial(kernel, total_steps), out_shape=(jax.Sha...]
where the time goes in v3:
time: 36.5 us; the launch traced here: 36.4 us
  Pallas kernels  33.3 us (91%)
  local copies, waits for them, and re-layouts  2.43 us (7%)
  between operations  0.64 us (2%)
    pallas_call x1, Pallas kernels, per_device(): pl.pallas_call(functools.partial(kernel, total_steps), out_shape=(jax.Sha...  33.3 us
    unnamed x4, local copies, waits for them, and re-layouts  2.43 us

profile of v3, /device:TPU:64, one launch (start us, length us, event | category | flops | bytes accessed | tf_op | source)
XLA Modules:
  0.0 36.4 jit_solution(14405061008207077071)
XLA Ops:
  0.6 33.3 %shard_map.75 = (bf16[64,1024]{1,0:T(8,128)(2,1)S(1)}, f32[8,4096]{1,0:T(8,128)S(1)}, f32[32,128]{1,0:T(8,128)S(1)}, f32[1,64]{1,0:T(1,128)S(1)}) custom-call(bf16[1024,512]{1,0:T(8,128)(2,1)} %rec_hbm.1, bf16[3,1536,512]{2,1,0:T(8,128)(2,1)} %bitcast.8, f32[3,512]{1,0:T(4,128)} %bias_hbm.1, bf16[64,512]{1,0:T(8,128)(2,1)} %bitcast.9), custom_call_target="tpu_custom_call" | custom-call | tf_op jit(solution)/shard_map/pallas_call | solution.py:461
  33.9 0.7 %copy.12 = bf16[1024,64]{0,1:T(8,128)(2,1)} copy(bf16[1024,64]{0,1:T(8,128)(2,1)S(1)} %bitcast.6) | data formatting | bytes 262144
  34.6 0.5 %copy.13 = f32[1,64]{1,0:T(1,128)} copy(f32[1,64]{1,0:T(1,128)S(1)} %get-tuple-element.17) | data formatting | bytes 512
  35.1 0.6 %copy.14 = f32[1,4096]{1,0:T(1,128)} copy(f32[1,4096]{1,0:T(1,128)S(1)} %bitcast.7) | data formatting | bytes 32768
  35.7 0.7 %copy.15 = f32[1,8,4096]{2,1,0:T(8,128)} copy(f32[1,8,4096]{2,1,0:T(8,128)S(1)} %bitcast.5) | data formatting | bytes 262144

commit v4 on v3

--- a/solution.py
+++ b/solution.py
@@ -16,7 +16,8 @@
 NZ = 4
 NY = 4
 TILE = 256
-PAY = 256 + 64 + 16
+PART = 128 + 16 + 8
+PAY = 128 + 32 + 16
 MESH = pl.DeviceIdType.MESH
 BF = jnp.bfloat16
 F32 = jnp.float32
@@ -57,9 +58,10 @@
     turned,
     partner_out,
     partner_in,
-    out_x,
+    out_1,
+    out_2,
+    out_low,
     in_x,
-    out_z,
     in_z,
     w_sem,
     small_sem,
@@ -74,6 +76,7 @@
     x_recv,
     z_send,
     z_recv,
+    z_ready,
 ):
     w = lax.axis_index("wide")
     n = lax.axis_index("narrow")
@@ -125,13 +128,18 @@
         pl.semaphore_signal(barrier, inc=1, device_id=y_peer(by), device_id_type=MESH)
         pl.semaphore_signal(barrier, inc=1, device_id=x_peer(by), device_id_type=MESH)
 
+        @pl.when(z + by < NZ)
+        def _():
+            pl.semaphore_signal(barrier, inc=1, device_id=z_peer(by), device_id_type=MESH)
+
+    pl.semaphore_signal(barrier, inc=1, device_id=partner, device_id_type=MESH)
+    greeted = has_left.astype(jnp.int32) + has_right.astype(jnp.int32) + 7 + z
+    pl.semaphore_wait(barrier, greeted)
+    for by in range(1, 4):
+
         @pl.when(z >= by)
         def _():
-            pl.semaphore_signal(barrier, inc=1, device_id=z_peer(-by), device_id_type=MESH)
-
-    pl.semaphore_signal(barrier, inc=1, device_id=partner, device_id_type=MESH)
-    copied_to = has_left.astype(jnp.int32) + has_right.astype(jnp.int32) + 7 + (NZ - 1 - z)
-    pl.semaphore_wait(barrier, copied_to)
+            pl.semaphore_signal(z_ready, inc=1, device_id=z_peer(-by), device_id_type=MESH)
 
     def remote(src, dst, send, recv, device):
         return pltpu.make_async_remote_copy(
@@ -346,90 +354,123 @@
             return rows + c_row * local2 + middle * s_row
 
         for r in range(4):
-            dst[pl.ds(64 * r, 64), :] = jnp.where(low_half, block(r), block(r + 4))
+            dst[r // 2, pl.ds(64 * (r % 2), 64), :] = jnp.where(low_half, block(r), block(r + 4))
+
+    def low_levels(dst):
+        pairs = packed_level2()
+        for half in range(2):
+            dst[half, pl.ds(128, 16), :] = pairs[16 * half : 16 * half + 16]
+            dst[half, pl.ds(144, 8), :] = delta
 
     third_rows(0, their_rows, partner_out)
-    partner_out[pl.ds(256, 32), :] = packed_level2()
-    partner_out[pl.ds(288, 8), :] = delta
+    low_levels(partner_out)
     swap = remote(partner_out, partner_in, p_send, p_recv, partner)
     swap.start()
 
     for slot in range(1, 4):
         add_rows(512, my_rows, slot, step_columns(slot))
     third_rows(512, my_rows, mine)
-    mine[pl.ds(256, 32), :] = packed_level2()
-    mine[pl.ds(288, 8), :] = delta
+    low_levels(mine)
     swap.wait_recv()
     mine[...] += partner_in[...]
 
-    def pack(dst, src):
-        dst[pl.ds(0, 256), :] = src[pl.ds(0, 256), :].astype(BF)
-        exact = src[pl.ds(256, 32), :]
+    def pack(dst, value):
+        dst[pl.ds(0, 128), :] = value[:128].astype(BF)
+        exact = value[128:144]
         high = exact.astype(BF)
-        dst[pl.ds(256, 32), :] = high
-        dst[pl.ds(288, 32), :] = (exact - high.astype(F32)).astype(BF)
-        exact = src[pl.ds(288, 8), :]
+        dst[pl.ds(128, 16), :] = high
+        dst[pl.ds(144, 16), :] = (exact - high.astype(F32)).astype(BF)
+        exact = value[144:152]
         high = exact.astype(BF).astype(F32)
-        dst[pl.ds(320, 16), :] = jnp.concatenate([high, exact - high], axis=0).astype(BF)
+        dst[pl.ds(160, 16), :] = jnp.concatenate([high, exact - high], axis=0).astype(BF)
 
     def unpack(src):
-        third = src[pl.ds(0, 256), :].astype(F32)
-        second = src[pl.ds(256, 32), :].astype(F32) + src[pl.ds(288, 32), :].astype(F32)
-        pair = src[pl.ds(320, 16), :].astype(F32)
+        second = src[pl.ds(128, 16), :].astype(F32) + src[pl.ds(144, 16), :].astype(F32)
+        pair = src[pl.ds(160, 16), :].astype(F32)
+        third = src[pl.ds(0, 128), :].astype(F32)
         return jnp.concatenate([third, second, pair[:8] + pair[8:]], axis=0)
 
-    pack(out_x, mine)
-    x_copies = []
-    for by in range(1, 4):
-        copy = remote(out_x, in_x.at[by - 1], x_send.at[by - 1], x_recv.at[by - 1], x_peer(by))
-        copy.start()
-        x_copies.append(copy)
-    for copy in x_copies:
-        copy.wait_recv()
+    def x_copy(src, half, by):
+        at = 3 * half + by - 1
+        return remote(src, in_x.at[at], x_send.at[at], x_recv.at[at], x_peer(by))
+
+    def z_copy(src, half, by):
+        at = 3 * half + by - 1
+        return remote(src, in_z.at[at], z_send.at[at], z_recv.at[at], z_peer(by))
+
+    def up_z(src, half):
+        for by in range(1, 4):
+
+            @pl.when(z + by < NZ)
+            def _():
+                z_copy(src, half, by).start()
+
+    def add_lower_z(dst, half):
+        for by in range(1, 4):
+
+            @pl.when(z >= by)
+            def _():
+                z_copy(out_2, half, by).wait_recv()
+                dst[...] += unpack(in_z.at[3 * half + by - 1])
+
+    pack(out_1.at[0], mine[0])
+    pack(out_1.at[1], mine[1])
+    for by in range(1, 4):
+        x_copy(out_1.at[0], 0, by).start()
+    @pl.when(z < NZ - 1)
+    def _():
+        pl.semaphore_wait(z_ready, NZ - 1 - z)
+
+    up_z(out_1.at[1], 1)
     swap.wait_send()
-    total = mine[...]
-    upto = mine[...]
-    for by in range(1, 4):
+
+    below = partner_out.at[1]
+    below[...] = jnp.zeros((PART, 128), F32)
+    add_lower_z(below, 1)
+    pack(out_low, below[...])
+    mine[1] += below[...]
+    pack(out_2.at[1], mine[1])
+    for by in range(1, 4):
+
+        @pl.when(x + by < NX)
+        def _():
+            x_copy(out_2.at[1], 1, by).start()
+
+        @pl.when(x + by >= NX)
+        def _():
+            x_copy(out_low, 1, by).start()
+
+    total = upto = mine[0]
+    for by in range(1, 4):
+        x_copy(out_1.at[0], 0, by).wait_recv()
         other = unpack(in_x.at[by - 1])
         total = total + other
         upto = upto + jnp.where(x >= by, other, jnp.zeros_like(other))
-    partner_out[...] = total
-    mine[...] = upto
-    pack(out_z, partner_out)
-    z_copies = []
-    for by in range(1, 4):
-        z_copies.append(
-            remote(out_z, in_z.at[by - 1], z_send.at[by - 1], z_recv.at[by - 1], z_peer(by))
-        )
-
-    for by in range(1, 4):
-
-        @pl.when(z + by < NZ)
-        def _():
-            z_copies[by - 1].start()
-
-    for by in range(1, 4):
-
-        @pl.when(z >= by)
-        def _():
-            z_copies[by - 1].wait_recv()
-            mine[...] += unpack(in_z.at[by - 1])
+    pack(out_2.at[0], total)
+    up_z(out_2.at[0], 0)
+    mine[0] = upto
+
+    for by in range(1, 4):
+        x_copy(out_low, 1, by).wait_recv()
+        mine[1] += unpack(in_x.at[3 + by - 1])
+    add_lower_z(mine.at[0], 0)
 
     scale = total_steps ** (-0.2)
-    ends = mine[pl.ds(288, 8), :]
+    ends = mine[0, pl.ds(144, 8), :]
     ends_k = jnp.broadcast_to(ends.T[:64, :1], (64, 128))
     first_ref[...] = ends[:1, :64] * scale
-    second_ref[...] = mine[pl.ds(256, 32), :] * scale**2
+    for half in range(2):
+        second_ref[pl.ds(16 * half, 16), :] = mine[half, pl.ds(128, 16), :] * scale**2
 
     def level2_row(r):
-        row = mine[pl.ds(256 + 4 * n + r // 2, 1), :]
+        row = mine[lax.div(n, 4), pl.ds(128 + 4 * lax.rem(n, 4) + r // 2, 1), :]
         other = pltpu.roll(row, 64, 1)
         low = low_half[:1]
         return jnp.where(low, row, other) if r % 2 == 0 else jnp.where(low, other, row)
 
     for r in range(4):
         row = jnp.where(low_half[:1], level2_row(r), level2_row(r + 4))
-        values = ((row * ends_k - mine[pl.ds(64 * r, 64), :]) * scale**3).T
+        values = ((row * ends_k - mine[r // 2, pl.ds(64 * (r % 2), 64), :]) * scale**3).T
         turned[pl.ds(r, 64, stride=8), :] = values[:64]
         turned[pl.ds(4 + r, 64, stride=8), :] = values[64:]
     for pair in range(32):
@@ -444,13 +485,26 @@
     def _():
         to_right.wait_send()
 
-    for copy in y_copies + x_copies:
+    for copy in y_copies:
         copy.wait_send()
     for by in range(1, 4):
-
-        @pl.when(z + by < NZ)
-        def _():
-            z_copies[by - 1].wait_send()
+        for half in range(2):
+            x_copy(out_low, half, by).wait_send()
+
+            @pl.when(z + by < NZ)
+            def _():
+                z_copy(out_low, half, by).wait_send()
+
+
+def emit(*refs):
+    copies = [
+        pltpu.make_async_copy(src, dst, refs[8].at[k])
+        for k, (src, dst) in enumerate(zip(refs[:4], refs[4:8]))
+    ]
+    for copy in copies:
+        copy.start()
+    for copy in copies:
+        copy.wait()
 
 
 def per_device(total_steps, recording, conv_weight, conv_bias, projection):
@@ -458,14 +512,15 @@
     hbm = pl.BlockSpec(memory_space=pltpu.HBM)
     operands = (recording, conv_weight.reshape(3, 3 * C, C), conv_bias, projection.T)
     operands = [pltpu.with_memory_space_constraint(a, pltpu.HBM) for a in operands]
-    path_points, third, second, first = pl.pallas_call(
+    out_shape = (
+        jax.ShapeDtypeStruct((PATH, TD), BF),
+        jax.ShapeDtypeStruct((8, PATH * PATH), F32),
+        jax.ShapeDtypeStruct((32, 128), F32),
+        jax.ShapeDtypeStruct((1, PATH), F32),
+    )
+    results = pl.pallas_call(
         functools.partial(kernel, total_steps),
-        out_shape=(
-            jax.ShapeDtypeStruct((PATH, TD), BF),
-            jax.ShapeDtypeStruct((8, PATH * PATH), F32),
-            jax.ShapeDtypeStruct((32, 128), F32),
-            jax.ShapeDtypeStruct((1, PATH), F32),
-        ),
+        out_shape=out_shape,
         in_specs=[hbm, hbm, hbm, hbm],
         out_specs=(vmem, vmem, vmem, vmem),
         scratch_shapes=[
@@ -481,14 +536,15 @@
             pltpu.VMEM((PATH, 128), F32),
             pltpu.VMEM((1168, 128), F32),
             pltpu.VMEM((64, 128), F32),
-            pltpu.VMEM((296, 128), F32),
+            pltpu.VMEM((2, PART, 128), F32),
             pltpu.VMEM((512, PATH), F32),
-            pltpu.VMEM((296, 128), F32),
-            pltpu.VMEM((296, 128), F32),
+            pltpu.VMEM((2, PART, 128), F32),
+            pltpu.VMEM((2, PART, 128), F32),
+            pltpu.VMEM((2, PAY, 128), BF),
+            pltpu.VMEM((2, PAY, 128), BF),
             pltpu.VMEM((PAY, 128), BF),
-            pltpu.VMEM((3, PAY, 128), BF),
-            pltpu.VMEM((PAY, 128), BF),
-            pltpu.VMEM((3, PAY, 128), BF),
+            pltpu.VMEM((6, PAY, 128), BF),
+            pltpu.VMEM((6, PAY, 128), BF),
             pltpu.SemaphoreType.DMA((3,)),
             pltpu.SemaphoreType.DMA((2,)),
             pltpu.SemaphoreType.DMA,
@@ -498,15 +554,24 @@
             pltpu.SemaphoreType.DMA((3, 4)),
             pltpu.SemaphoreType.DMA,
             pltpu.SemaphoreType.DMA,
-            pltpu.SemaphoreType.DMA((3,)),
-            pltpu.SemaphoreType.DMA((3,)),
-            pltpu.SemaphoreType.DMA((3,)),
-            pltpu.SemaphoreType.DMA((3,)),
+            pltpu.SemaphoreType.DMA((6,)),
+            pltpu.SemaphoreType.DMA((6,)),
+            pltpu.SemaphoreType.DMA((6,)),
+            pltpu.SemaphoreType.DMA((6,)),
+            pltpu.SemaphoreType.REGULAR,
         ],
         compiler_params=pltpu.CompilerParams(
             collective_id=0, has_side_effects=True, vmem_limit_bytes=48 << 20
         ),
     )(*operands)
+    path_points, third, second, first = pl.pallas_call(
+        emit,
+        out_shape=out_shape,
+        in_specs=[vmem] * 4,
+        out_specs=[hbm] * 4,
+        scratch_shapes=[pltpu.SemaphoreType.DMA((4,))],
+        compiler_params=pltpu.CompilerParams(vmem_limit_bytes=1 << 20),
+    )(*results)
     return path_points.T, first, second.reshape(1, PATH * PATH), third[None]
 
 

time: 36.5 us -> 32.5 us (0.89)
  local copies, waits for them, and re-layouts: 2.43 us -> 0 us
  Pallas kernels: 33.3 us -> 31.8 us
    unnamed x4 -> x0, local copies, waits for them, and re-layouts: 2.43 us -> none
    pallas_call x1 -> x2, Pallas kernels: 33.3 us -> 31.8 us  [the longest x1 31 us: per_device(): pl.pallas_call(functools.partial(kernel, total_steps), out_shape=out_shap...]
where the time goes in v4:
time: 32.5 us; the launch traced here: 32.4 us
  Pallas kernels  31.8 us (98%)
  between operations  0.64 us (2%)
    pallas_call x1, Pallas kernels, per_device(): pl.pallas_call(functools.partial(kernel, total_steps), out_shape=out_shap...  31 us
    pallas_call x1, Pallas kernels, per_device(): pl.pallas_call(emit, out_shape=out_shape, in_specs=[vmem] * 4, out_specs=...  0.74 us

profile of v4, /device:TPU:64, one launch (start us, length us, event | category | flops | bytes accessed | tf_op | source)
XLA Modules:
  0.0 32.4 jit_solution(16949800189195726716)
XLA Ops:
  0.6 31.0 %shard_map.75 = (bf16[64,1024]{1,0:T(8,128)(2,1)S(1)}, f32[8,4096]{1,0:T(8,128)S(1)}, f32[32,128]{1,0:T(8,128)S(1)}, f32[1,64]{1,0:T(1,128)S(1)}) custom-call(bf16[1024,512]{1,0:T(8,128)(2,1)} %rec_hbm.1, bf16[3,1536,512]{2,1,0:T(8,128)(2,1)} %bitcast.5, f32[3,512]{1,0:T(4,128)} %bias_hbm.1, bf16[64,512]{1,0:T(8,128)(2,1)} %bitcast.6), custom_call_target="tpu_custom_call" | custom-call | tf_op jit(solution)/shard_map/pallas_call | solution.py:521
  31.7 0.7 %shard_map.76 = (bf16[64,1024]{1,0:T(8,128)(2,1)}, f32[8,4096]{1,0:T(8,128)}, f32[32,128]{1,0:T(8,128)}, f32[1,64]{1,0:T(1,128)}) custom-call(bf16[64,1024]{1,0:T(8,128)(2,1)S(1)} %get-tuple-element.12.refs_0_, f32[8,4096]{1,0:T(8,128)S(1)} %get-tuple-element.13.refs_1_, f32[32,128]{1,0:T(8,128)S(1)} %get-tuple-element.14.refs_2_, ...), custom_call_target="tpu_custom_call" | custom-call | tf_op jit(solution)/shard_map/pallas_call | solution.py:567

commit v5 on v4

--- a/solution.py
+++ b/solution.py
@@ -110,9 +110,7 @@
     ]
     own_copy.start()
     small_copies[0].start()
-    for copy in weight_copies:
-        copy.start()
-    small_copies[1].start()
+    weight_copies[0].start()
 
     barrier = pltpu.get_barrier_semaphore()
 
@@ -198,6 +196,9 @@
     own_copy.wait()
     small_copies[0].wait()
     weight_copies[0].wait()
+    weight_copies[1].start()
+    small_copies[1].start()
+    weight_copies[2].start()
     for i in range(1, 7):
         put(h1, conv(0, h0, *tiles[i]), i)
 
@@ -253,17 +254,18 @@
     weight_copies[1].wait()
     put(h2, conv(1, h1, *tiles[0]), 0)
     put(h2, conv(1, h1, *tiles[1]), 1)
+    put(h2, conv(1, h1, *tiles[2]), 2)
     weight_copies[2].wait()
     small_copies[1].wait()
-    finish(0)
-    for i in range(2, 8):
+    for i in range(3, 8):
         put(h2, conv(1, h1, *tiles[i]), i)
-        finish(i - 1)
+        finish(i - 3)
+    finish(5)
+    known = seg[0, :, pl.ds(128, 640)].astype(F32)
+    mean = jnp.sum(known, axis=1, keepdims=True) * (1.0 / 640)
+    centre[...] = jnp.broadcast_to(mean, (PATH, 128))
+    finish(6)
     finish(7)
-
-    own_points = seg[0, :, pl.ds(128, TD)].astype(F32)
-    mean = jnp.sum(own_points, axis=1, keepdims=True) * (1.0 / TD)
-    centre[...] = jnp.broadcast_to(mean, (PATH, 128))
 
     def prepare(slot, t, buf):
         window = seg[slot, :, pl.ds(TILE * t, 384)].astype(F32)
@@ -279,13 +281,14 @@
         return jnp.concatenate([high, low], axis=0)
 
     def add_rows(at, row_begin, buf, columns):
-        m = mid[buf]
-        d = step[buf] * (1.0 / 12.0)
-        rows = []
-        for r in range(8):
-            m_row = mid[buf, pl.ds(row_begin + r, 1), :]
-            d_row = step[buf, pl.ds(row_begin + r, 1), :]
-            rows.append((m_row * m + d_row * d).astype(BF))
+        m = mid[buf].astype(BF)
+        d = (step[buf] * (1.0 / 12.0)).astype(BF)
+
+        def spread(ref, r):
+            row = jnp.broadcast_to(ref[buf, pl.ds(row_begin + r, 1), :], (16, TILE)).astype(BF)
+            return jnp.concatenate([row] * 4, axis=0)
+
+        rows = [spread(mid, r) * m + spread(step, r) * d for r in range(8)]
         acc[pl.ds(at, 512), :] += nt_dot(jnp.concatenate(rows, axis=0), columns)
 
     def add_level2(buf, columns):
@@ -317,12 +320,13 @@
             add_level2(at % 4, columns)
             add_rows(512, my_rows, at % 4, columns)
 
-    everything([(0, t) for t in range(4)])
+    steps = [(0, t) for t in range(4)]
     for group in ((0, 1), (2,)):
         for t in group:
             for slot in range(1, 4):
                 wait_tile(slot, t)
-        everything([(slot, t) for t in group for slot in range(1, 4)])
+        everything(steps + [(slot, t) for t in group for slot in range(1, 4)])
+        steps = []
     for slot in range(1, 4):
         wait_tile(slot, 3)
     for slot in range(1, 4):

time: 32.5 us -> 32.7 us (level)
  no operation moved by 1% of the time
where the time goes in v5:
time: 32.7 us; the launch traced here: 32.6 us
  Pallas kernels  32 us (98%)
  between operations  0.64 us (2%)
    pallas_call x1, Pallas kernels, per_device(): pl.pallas_call(functools.partial(kernel, total_steps), out_shape=out_shap...  31.2 us
    pallas_call x1, Pallas kernels, per_device(): pl.pallas_call(emit, out_shape=out_shape, in_specs=[vmem] * 4, out_specs=...  0.74 us

profile of v5, /device:TPU:64, one launch (start us, length us, event | category | flops | bytes accessed | tf_op | source)
XLA Modules:
  0.0 32.6 jit_solution(14917358413772452227)
XLA Ops:
  0.6 31.2 %shard_map.75 = (bf16[64,1024]{1,0:T(8,128)(2,1)S(1)}, f32[8,4096]{1,0:T(8,128)S(1)}, f32[32,128]{1,0:T(8,128)S(1)}, f32[1,64]{1,0:T(1,128)S(1)}) custom-call(bf16[1024,512]{1,0:T(8,128)(2,1)} %rec_hbm.1, bf16[3,1536,512]{2,1,0:T(8,128)(2,1)} %bitcast.5, f32[3,512]{1,0:T(4,128)} %bias_hbm.1, bf16[64,512]{1,0:T(8,128)(2,1)} %bitcast.6), custom_call_target="tpu_custom_call" | custom-call | tf_op jit(solution)/shard_map/pallas_call | solution.py:525
  31.9 0.7 %shard_map.76 = (bf16[64,1024]{1,0:T(8,128)(2,1)}, f32[8,4096]{1,0:T(8,128)}, f32[32,128]{1,0:T(8,128)}, f32[1,64]{1,0:T(1,128)}) custom-call(bf16[64,1024]{1,0:T(8,128)(2,1)S(1)} %get-tuple-element.12.refs_0_, f32[8,4096]{1,0:T(8,128)S(1)} %get-tuple-element.13.refs_1_, f32[32,128]{1,0:T(8,128)S(1)} %get-tuple-element.14.refs_2_, ...), custom_call_target="tpu_custom_call" | custom-call | tf_op jit(solution)/shard_map/pallas_call | solution.py:571

commit v6 on v5

--- a/solution.py
+++ b/solution.py
@@ -123,7 +123,8 @@
         pl.semaphore_signal(barrier, inc=1, device_id=right, device_id_type=MESH)
 
     for by in range(1, 4):
-        pl.semaphore_signal(barrier, inc=1, device_id=y_peer(by), device_id_type=MESH)
+        if by != 2:
+            pl.semaphore_signal(barrier, inc=1, device_id=y_peer(by), device_id_type=MESH)
         pl.semaphore_signal(barrier, inc=1, device_id=x_peer(by), device_id_type=MESH)
 
         @pl.when(z + by < NZ)
@@ -131,7 +132,7 @@
             pl.semaphore_signal(barrier, inc=1, device_id=z_peer(by), device_id_type=MESH)
 
     pl.semaphore_signal(barrier, inc=1, device_id=partner, device_id_type=MESH)
-    greeted = has_left.astype(jnp.int32) + has_right.astype(jnp.int32) + 7 + z
+    greeted = has_left.astype(jnp.int32) + has_right.astype(jnp.int32) + 6 + z
     pl.semaphore_wait(barrier, greeted)
     for by in range(1, 4):
 
@@ -223,18 +224,32 @@
 
     y_copies = []
 
+    def tile_copy(way, t):
+        begin, end = (0, 384) if t == 0 else (128 + TILE * t, 128 + TILE * (t + 1))
+        half = end - 128
+        lanes = [(begin, end), (begin, end), (begin, half), (half, end)][way]
+        lanes = pl.ds(lanes[0], lanes[1] - lanes[0])
+        return remote(
+            seg.at[(0, 0, 1, 2)[way], :, lanes],
+            seg.at[(1, 2, 3, 3)[way], :, lanes],
+            y_send.at[way, t],
+            y_recv.at[way, t],
+            y_peer((1, 3, 1, 3)[way]),
+        )
+
+    def send(way, t):
+        copy = tile_copy(way, t)
+        copy.start()
+        y_copies.append(copy)
+
     def send_tile(t):
-        lanes = pl.ds(0, 384) if t == 0 else pl.ds(128 + TILE * t, TILE)
-        for slot, by in ((1, 1), (2, 3), (3, 2)):
-            copy = remote(
-                seg.at[0, :, lanes],
-                seg.at[slot, :, lanes],
-                y_send.at[slot - 1, t],
-                y_recv.at[slot - 1, t],
-                y_peer(by),
-            )
-            copy.start()
-            y_copies.append(copy)
+        send(0, t)
+        send(1, t)
+
+    def relay(t):
+        for way in (0, 1):
+            tile_copy(way, t).wait_recv()
+            send(way + 2, t)
 
     def finish(i):
         begin, end = tiles[i]
@@ -250,17 +265,17 @@
         seg[0, :, pl.ds(128 + 128 * i, 128)] = points
         if i % 2 == 1:
             send_tile(i // 2)
+            if i > 1:
+                relay(i // 2 - 1)
 
     weight_copies[1].wait()
     put(h2, conv(1, h1, *tiles[0]), 0)
     put(h2, conv(1, h1, *tiles[1]), 1)
-    put(h2, conv(1, h1, *tiles[2]), 2)
     weight_copies[2].wait()
     small_copies[1].wait()
-    for i in range(3, 8):
+    for i in range(2, 8):
         put(h2, conv(1, h1, *tiles[i]), i)
-        finish(i - 3)
-    finish(5)
+        finish(i - 2)
     known = seg[0, :, pl.ds(128, 640)].astype(F32)
     mean = jnp.sum(known, axis=1, keepdims=True) * (1.0 / 640)
     centre[...] = jnp.broadcast_to(mean, (PATH, 128))
@@ -302,15 +317,9 @@
     my_rows = y * 16 + core * 8
     acc[...] = jnp.zeros_like(acc)
 
-    def wait_tile(slot, t):
-        lanes = pl.ds(0, 384) if t == 0 else pl.ds(128 + TILE * t, TILE)
-        remote(
-            seg.at[0, :, lanes],
-            seg.at[slot, :, lanes],
-            y_send.at[slot - 1, t],
-            y_recv.at[slot - 1, t],
-            y_peer(1),
-        ).wait_recv()
+    def wait_relayed(t):
+        tile_copy(2, t).wait_recv()
+        tile_copy(3, t).wait_recv()
 
     def everything(steps):
         for at, (slot, t) in enumerate(steps):
@@ -320,20 +329,23 @@
             add_level2(at % 4, columns)
             add_rows(512, my_rows, at % 4, columns)
 
-    steps = [(0, t) for t in range(4)]
-    for group in ((0, 1), (2,)):
-        for t in group:
-            for slot in range(1, 4):
-                wait_tile(slot, t)
-        everything(steps + [(slot, t) for t in group for slot in range(1, 4)])
-        steps = []
-    for slot in range(1, 4):
-        wait_tile(slot, 3)
-    for slot in range(1, 4):
+    wait_relayed(0)
+    everything([(0, t) for t in range(4)] + [(slot, 0) for slot in range(1, 4)] + [(1, 1)])
+    relay(3)
+    wait_relayed(1)
+    wait_relayed(2)
+    everything([(2, 1), (3, 1), (1, 2), (2, 2), (3, 2)])
+
+    def their_step(slot):
         prepare(slot, 3, slot)
         columns = step_columns(slot)
         add_rows(0, their_rows, slot, columns)
         add_level2(slot, columns)
+
+    their_step(1)
+    their_step(2)
+    wait_relayed(3)
+    their_step(3)
 
     low_half = lax.broadcasted_iota(jnp.int32, (64, 128), 1) < 64
 
@@ -554,8 +566,8 @@
             pltpu.SemaphoreType.DMA,
             pltpu.SemaphoreType.DMA((2,)),
             pltpu.SemaphoreType.DMA((2,)),
-            pltpu.SemaphoreType.DMA((3, 4)),
-            pltpu.SemaphoreType.DMA((3, 4)),
+            pltpu.SemaphoreType.DMA((4, 4)),
+            pltpu.SemaphoreType.DMA((4, 4)),
             pltpu.SemaphoreType.DMA,
             pltpu.SemaphoreType.DMA,
             pltpu.SemaphoreType.DMA((6,)),

time: 32.7 us -> 35.5 us (1.086)
  Pallas kernels: 32 us -> 34.8 us
    pallas_call x1, Pallas kernels: 31.2 us -> 34 us  [per_device(): pl.pallas_call(functools.partial(kernel, total_steps), out_shape=out_shap...]
where the time goes in v6:
time: 35.5 us; the launch traced here: 35.4 us
  Pallas kernels  34.8 us (98%)
  between operations  0.64 us (2%)
    pallas_call x1, Pallas kernels, per_device(): pl.pallas_call(functools.partial(kernel, total_steps), out_shape=out_shap...  34 us
    pallas_call x1, Pallas kernels, per_device(): pl.pallas_call(emit, out_shape=out_shape, in_specs=[vmem] * 4, out_specs=...  0.74 us

profile of v6, /device:TPU:64, one launch (start us, length us, event | category | flops | bytes accessed | tf_op | source)
XLA Modules:
  0.0 35.4 jit_solution(17384621143300422369)
XLA Ops:
  0.6 34.0 %shard_map.75 = (bf16[64,1024]{1,0:T(8,128)(2,1)S(1)}, f32[8,4096]{1,0:T(8,128)S(1)}, f32[32,128]{1,0:T(8,128)S(1)}, f32[1,64]{1,0:T(1,128)S(1)}) custom-call(bf16[1024,512]{1,0:T(8,128)(2,1)} %rec_hbm.1, bf16[3,1536,512]{2,1,0:T(8,128)(2,1)} %bitcast.5, f32[3,512]{1,0:T(4,128)} %bias_hbm.1, bf16[64,512]{1,0:T(8,128)(2,1)} %bitcast.6), custom_call_target="tpu_custom_call" | custom-call | tf_op jit(solution)/shard_map/pallas_call | solution.py:537
  34.7 0.7 %shard_map.76 = (bf16[64,1024]{1,0:T(8,128)(2,1)}, f32[8,4096]{1,0:T(8,128)}, f32[32,128]{1,0:T(8,128)}, f32[1,64]{1,0:T(1,128)}) custom-call(bf16[64,1024]{1,0:T(8,128)(2,1)S(1)} %get-tuple-element.12.refs_0_, f32[8,4096]{1,0:T(8,128)S(1)} %get-tuple-element.13.refs_1_, f32[32,128]{1,0:T(8,128)S(1)} %get-tuple-element.14.refs_2_, ...), custom_call_target="tpu_custom_call" | custom-call | tf_op jit(solution)/shard_map/pallas_call | solution.py:583

commit v7 on v6

--- a/solution.py
+++ b/solution.py
@@ -265,8 +265,8 @@
         seg[0, :, pl.ds(128 + 128 * i, 128)] = points
         if i % 2 == 1:
             send_tile(i // 2)
-            if i > 1:
-                relay(i // 2 - 1)
+            if i > 3:
+                relay(i // 2 - 2)
 
     weight_copies[1].wait()
     put(h2, conv(1, h1, *tiles[0]), 0)
@@ -329,12 +329,15 @@
             add_level2(at % 4, columns)
             add_rows(512, my_rows, at % 4, columns)
 
+    everything([(0, t) for t in range(4)])
+    relay(2)
+    everything([(1, 0), (2, 0), (1, 1), (2, 1)])
+    relay(3)
     wait_relayed(0)
-    everything([(0, t) for t in range(4)] + [(slot, 0) for slot in range(1, 4)] + [(1, 1)])
-    relay(3)
     wait_relayed(1)
+    everything([(1, 2), (2, 2), (3, 0), (3, 1), (1, 3), (2, 3)])
     wait_relayed(2)
-    everything([(2, 1), (3, 1), (1, 2), (2, 2), (3, 2)])
+    everything([(3, 2)])
 
     def their_step(slot):
         prepare(slot, 3, slot)
@@ -342,8 +345,6 @@
         add_rows(0, their_rows, slot, columns)
         add_level2(slot, columns)
 
-    their_step(1)
-    their_step(2)
     wait_relayed(3)
     their_step(3)
 
@@ -383,8 +384,7 @@
     swap = remote(partner_out, partner_in, p_send, p_recv, partner)
     swap.start()
 
-    for slot in range(1, 4):
-        add_rows(512, my_rows, slot, step_columns(slot))
+    add_rows(512, my_rows, 3, step_columns(3))
     third_rows(512, my_rows, mine)
     low_levels(mine)
     swap.wait_recv()

time: 35.5 us -> 32.9 us (0.927)
  Pallas kernels: 34.8 us -> 32 us
    pallas_call x1, Pallas kernels: 34 us -> 31.2 us  [per_device(): pl.pallas_call(functools.partial(kernel, total_steps), out_shape=out_shap...]
where the time goes in v7:
time: 32.9 us; the launch traced here: 32.6 us
  Pallas kernels  32 us (97%)
  between operations  0.64 us (2%)
    pallas_call x1, Pallas kernels, per_device(): pl.pallas_call(functools.partial(kernel, total_steps), out_shape=out_shap...  31.2 us
    pallas_call x1, Pallas kernels, per_device(): pl.pallas_call(emit, out_shape=out_shape, in_specs=[vmem] * 4, out_specs=...  0.74 us

profile of v7, /device:TPU:64, one launch (start us, length us, event | category | flops | bytes accessed | tf_op | source)
XLA Modules:
  0.0 32.6 jit_solution(10197767682021164596)
XLA Ops:
  0.6 31.2 %shard_map.75 = (bf16[64,1024]{1,0:T(8,128)(2,1)S(1)}, f32[8,4096]{1,0:T(8,128)S(1)}, f32[32,128]{1,0:T(8,128)S(1)}, f32[1,64]{1,0:T(1,128)S(1)}) custom-call(bf16[1024,512]{1,0:T(8,128)(2,1)} %rec_hbm.1, bf16[3,1536,512]{2,1,0:T(8,128)(2,1)} %bitcast.5, f32[3,512]{1,0:T(4,128)} %bias_hbm.1, bf16[64,512]{1,0:T(8,128)(2,1)} %bitcast.6), custom_call_target="tpu_custom_call" | custom-call | tf_op jit(solution)/shard_map/pallas_call | solution.py:537
  31.9 0.7 %shard_map.76 = (bf16[64,1024]{1,0:T(8,128)(2,1)}, f32[8,4096]{1,0:T(8,128)}, f32[32,128]{1,0:T(8,128)}, f32[1,64]{1,0:T(1,128)}) custom-call(bf16[64,1024]{1,0:T(8,128)(2,1)S(1)} %get-tuple-element.12.refs_0_, f32[8,4096]{1,0:T(8,128)S(1)} %get-tuple-element.13.refs_1_, f32[32,128]{1,0:T(8,128)S(1)} %get-tuple-element.14.refs_2_, ...), custom_call_target="tpu_custom_call" | custom-call | tf_op jit(solution)/shard_map/pallas_call | solution.py:583

commit v8 on v7

--- a/solution.py
+++ b/solution.py
@@ -123,8 +123,7 @@
         pl.semaphore_signal(barrier, inc=1, device_id=right, device_id_type=MESH)
 
     for by in range(1, 4):
-        if by != 2:
-            pl.semaphore_signal(barrier, inc=1, device_id=y_peer(by), device_id_type=MESH)
+        pl.semaphore_signal(barrier, inc=1, device_id=y_peer(by), device_id_type=MESH)
         pl.semaphore_signal(barrier, inc=1, device_id=x_peer(by), device_id_type=MESH)
 
         @pl.when(z + by < NZ)
@@ -132,7 +131,7 @@
             pl.semaphore_signal(barrier, inc=1, device_id=z_peer(by), device_id_type=MESH)
 
     pl.semaphore_signal(barrier, inc=1, device_id=partner, device_id_type=MESH)
-    greeted = has_left.astype(jnp.int32) + has_right.astype(jnp.int32) + 6 + z
+    greeted = has_left.astype(jnp.int32) + has_right.astype(jnp.int32) + 7 + z
     pl.semaphore_wait(barrier, greeted)
     for by in range(1, 4):
 
@@ -227,14 +226,15 @@
     def tile_copy(way, t):
         begin, end = (0, 384) if t == 0 else (128 + TILE * t, 128 + TILE * (t + 1))
         half = end - 128
-        lanes = [(begin, end), (begin, end), (begin, half), (half, end)][way]
+        lanes = {2: (begin, half), 3: (half, end)}.get(way, (begin, end))
         lanes = pl.ds(lanes[0], lanes[1] - lanes[0])
+        at = way if way < 4 else 2
         return remote(
-            seg.at[(0, 0, 1, 2)[way], :, lanes],
-            seg.at[(1, 2, 3, 3)[way], :, lanes],
-            y_send.at[way, t],
-            y_recv.at[way, t],
-            y_peer((1, 3, 1, 3)[way]),
+            seg.at[(0, 0, 1, 2, 0)[way], :, lanes],
+            seg.at[(1, 2, 3, 3, 3)[way], :, lanes],
+            y_send.at[at, t],
+            y_recv.at[at, t],
+            y_peer((1, 3, 1, 3, 2)[way]),
         )
 
     def send(way, t):
@@ -243,6 +243,8 @@
         y_copies.append(copy)
 
     def send_tile(t):
+        if t > 1:
+            send(4, t)
         send(0, t)
         send(1, t)
 
@@ -329,15 +331,14 @@
             add_level2(at % 4, columns)
             add_rows(512, my_rows, at % 4, columns)
 
-    everything([(0, t) for t in range(4)])
-    relay(2)
-    everything([(1, 0), (2, 0), (1, 1), (2, 1)])
-    relay(3)
+    everything([(0, t) for t in range(4)] + [(slot, t) for t in range(2) for slot in (1, 2)])
     wait_relayed(0)
     wait_relayed(1)
-    everything([(1, 2), (2, 2), (3, 0), (3, 1), (1, 3), (2, 3)])
-    wait_relayed(2)
-    everything([(3, 2)])
+    for way in (0, 1, 4):
+        tile_copy(way, 2).wait_recv()
+    everything([(3, 0), (3, 1), (1, 2), (2, 2), (3, 2)])
+    for way in (0, 1, 4):
+        tile_copy(way, 3).wait_recv()
 
     def their_step(slot):
         prepare(slot, 3, slot)
@@ -345,8 +346,8 @@
         add_rows(0, their_rows, slot, columns)
         add_level2(slot, columns)
 
-    wait_relayed(3)
-    their_step(3)
+    for slot in range(1, 4):
+        their_step(slot)
 
     low_half = lax.broadcasted_iota(jnp.int32, (64, 128), 1) < 64
 
@@ -384,7 +385,8 @@
     swap = remote(partner_out, partner_in, p_send, p_recv, partner)
     swap.start()
 
-    add_rows(512, my_rows, 3, step_columns(3))
+    for slot in range(1, 4):
+        add_rows(512, my_rows, slot, step_columns(slot))
     third_rows(512, my_rows, mine)
     low_levels(mine)
     swap.wait_recv()

time: 32.9 us -> 33.5 us (1.018)
  no operation moved by 1% of the time
where the time goes in v8:
time: 33.5 us; the launch traced here: 32.9 us
  Pallas kernels  32.3 us (96%)
  between operations  0.64 us (2%)
    pallas_call x1, Pallas kernels, per_device(): pl.pallas_call(functools.partial(kernel, total_steps), out_shape=out_shap...  31.6 us
    pallas_call x1, Pallas kernels, per_device(): pl.pallas_call(emit, out_shape=out_shape, in_specs=[vmem] * 4, out_specs=...  0.74 us

profile of v8, /device:TPU:64, one launch (start us, length us, event | category | flops | bytes accessed | tf_op | source)
XLA Modules:
  0.0 32.9 jit_solution(4661365239816034883)
XLA Ops:
  0.6 31.6 %shard_map.75 = (bf16[64,1024]{1,0:T(8,128)(2,1)S(1)}, f32[8,4096]{1,0:T(8,128)S(1)}, f32[32,128]{1,0:T(8,128)S(1)}, f32[1,64]{1,0:T(1,128)S(1)}) custom-call(bf16[1024,512]{1,0:T(8,128)(2,1)} %rec_hbm.1, bf16[3,1536,512]{2,1,0:T(8,128)(2,1)} %bitcast.5, f32[3,512]{1,0:T(4,128)} %bias_hbm.1, bf16[64,512]{1,0:T(8,128)(2,1)} %bitcast.6), custom_call_target="tpu_custom_call" | custom-call | tf_op jit(solution)/shard_map/pallas_call | solution.py:539
  32.2 0.7 %shard_map.76 = (bf16[64,1024]{1,0:T(8,128)(2,1)}, f32[8,4096]{1,0:T(8,128)}, f32[32,128]{1,0:T(8,128)}, f32[1,64]{1,0:T(1,128)}) custom-call(bf16[64,1024]{1,0:T(8,128)(2,1)S(1)} %get-tuple-element.12.refs_0_, f32[8,4096]{1,0:T(8,128)S(1)} %get-tuple-element.13.refs_1_, f32[32,128]{1,0:T(8,128)S(1)} %get-tuple-element.14.refs_2_, ...), custom_call_target="tpu_custom_call" | custom-call | tf_op jit(solution)/shard_map/pallas_call | solution.py:585

commit v9 on v5

--- a/solution.py
+++ b/solution.py
@@ -199,7 +199,7 @@
     weight_copies[1].start()
     small_copies[1].start()
     weight_copies[2].start()
-    for i in range(1, 7):
+    for i in range(1, 6):
         put(h1, conv(0, h0, *tiles[i]), i)
 
     @pl.when(has_left)
@@ -218,7 +218,6 @@
     def _():
         h0[pl.ds(OFF + TD, 16), :] = jnp.zeros((16, C), BF)
 
-    put(h1, conv(0, h0, *tiles[7]), 7)
     put(h1, conv(0, h0, *tiles[0]), 0)
 
     y_copies = []
@@ -251,15 +250,29 @@
         if i % 2 == 1:
             send_tile(i // 2)
 
+    def layer_1(*which):
+        for i in which:
+            put(h1, conv(0, h0, *tiles[i]), i)
+
+    def layer_2(*which):
+        for i in which:
+            put(h2, conv(1, h1, *tiles[i]), i)
+
     weight_copies[1].wait()
-    put(h2, conv(1, h1, *tiles[0]), 0)
-    put(h2, conv(1, h1, *tiles[1]), 1)
-    put(h2, conv(1, h1, *tiles[2]), 2)
+    layer_2(0, 1, 2)
     weight_copies[2].wait()
     small_copies[1].wait()
-    for i in range(3, 8):
-        put(h2, conv(1, h1, *tiles[i]), i)
-        finish(i - 3)
+    finish(0)
+    layer_2(3)
+    finish(1)
+    layer_2(4)
+    finish(2)
+    layer_1(6)
+    finish(3)
+    layer_1(7)
+    layer_2(5, 6)
+    finish(4)
+    layer_2(7)
     finish(5)
     known = seg[0, :, pl.ds(128, 640)].astype(F32)
     mean = jnp.sum(known, axis=1, keepdims=True) * (1.0 / 640)

time: 32.7 us -> 32.7 us (level)
  no operation moved by 1% of the time
where the time goes in v9:
time: 32.7 us; the launch traced here: 32.6 us
  Pallas kernels  31.9 us (98%)
  between operations  0.64 us (2%)
    pallas_call x1, Pallas kernels, per_device(): pl.pallas_call(functools.partial(kernel, total_steps), out_shape=out_shap...  31.2 us
    pallas_call x1, Pallas kernels, per_device(): pl.pallas_call(emit, out_shape=out_shape, in_specs=[vmem] * 4, out_specs=...  0.74 us

profile of v9, /device:TPU:64, one launch (start us, length us, event | category | flops | bytes accessed | tf_op | source)
XLA Modules:
  0.0 32.6 jit_solution(17243573359760377000)
XLA Ops:
  0.6 31.2 %shard_map.75 = (bf16[64,1024]{1,0:T(8,128)(2,1)S(1)}, f32[8,4096]{1,0:T(8,128)S(1)}, f32[32,128]{1,0:T(8,128)S(1)}, f32[1,64]{1,0:T(1,128)S(1)}) custom-call(bf16[1024,512]{1,0:T(8,128)(2,1)} %rec_hbm.1, bf16[3,1536,512]{2,1,0:T(8,128)(2,1)} %bitcast.5, f32[3,512]{1,0:T(4,128)} %bias_hbm.1, bf16[64,512]{1,0:T(8,128)(2,1)} %bitcast.6), custom_call_target="tpu_custom_call" | custom-call | tf_op jit(solution)/shard_map/pallas_call | solution.py:538
  31.8 0.7 %shard_map.76 = (bf16[64,1024]{1,0:T(8,128)(2,1)}, f32[8,4096]{1,0:T(8,128)}, f32[32,128]{1,0:T(8,128)}, f32[1,64]{1,0:T(1,128)}) custom-call(bf16[64,1024]{1,0:T(8,128)(2,1)S(1)} %get-tuple-element.12.refs_0_, f32[8,4096]{1,0:T(8,128)S(1)} %get-tuple-element.13.refs_1_, f32[32,128]{1,0:T(8,128)S(1)} %get-tuple-element.14.refs_2_, ...), custom_call_target="tpu_custom_call" | custom-call | tf_op jit(solution)/shard_map/pallas_call | solution.py:584

commit v10 on v9

--- a/solution.py
+++ b/solution.py
@@ -221,9 +221,10 @@
     put(h1, conv(0, h0, *tiles[0]), 0)
 
     y_copies = []
+    sent_lanes = (pl.ds(0, 640), pl.ds(640, TILE), pl.ds(896, TILE))
 
     def send_tile(t):
-        lanes = pl.ds(0, 384) if t == 0 else pl.ds(128 + TILE * t, TILE)
+        lanes = sent_lanes[t]
         for slot, by in ((1, 1), (2, 3), (3, 2)):
             copy = remote(
                 seg.at[0, :, lanes],
@@ -247,8 +248,8 @@
         points = points.astype(BF)
         path_ref[:, pl.ds(128 * i, 128)] = points
         seg[0, :, pl.ds(128 + 128 * i, 128)] = points
-        if i % 2 == 1:
-            send_tile(i // 2)
+        if i in (3, 5, 7):
+            send_tile(i // 2 - 1)
 
     def layer_1(*which):
         for i in which:
@@ -316,7 +317,7 @@
     acc[...] = jnp.zeros_like(acc)
 
     def wait_tile(slot, t):
-        lanes = pl.ds(0, 384) if t == 0 else pl.ds(128 + TILE * t, TILE)
+        lanes = sent_lanes[t]
         remote(
             seg.at[0, :, lanes],
             seg.at[slot, :, lanes],
@@ -334,14 +335,13 @@
             add_rows(512, my_rows, at % 4, columns)
 
     steps = [(0, t) for t in range(4)]
-    for group in ((0, 1), (2,)):
-        for t in group:
-            for slot in range(1, 4):
-                wait_tile(slot, t)
+    for sent, group in enumerate(((0, 1), (2,))):
+        for slot in range(1, 4):
+            wait_tile(slot, sent)
         everything(steps + [(slot, t) for t in group for slot in range(1, 4)])
         steps = []
     for slot in range(1, 4):
-        wait_tile(slot, 3)
+        wait_tile(slot, 2)
     for slot in range(1, 4):
         prepare(slot, 3, slot)
         columns = step_columns(slot)
@@ -567,8 +567,8 @@
             pltpu.SemaphoreType.DMA,
             pltpu.SemaphoreType.DMA((2,)),
             pltpu.SemaphoreType.DMA((2,)),
-            pltpu.SemaphoreType.DMA((3, 4)),
-            pltpu.SemaphoreType.DMA((3, 4)),
+            pltpu.SemaphoreType.DMA((3, 3)),
+            pltpu.SemaphoreType.DMA((3, 3)),
             pltpu.SemaphoreType.DMA,
             pltpu.SemaphoreType.DMA,
             pltpu.SemaphoreType.DMA((6,)),

time: 32.7 us -> 33.5 us (1.024)
  Pallas kernels: 31.9 us -> 32.7 us
    pallas_call x1, Pallas kernels: 31.2 us -> 32 us  [per_device(): pl.pallas_call(functools.partial(kernel, total_steps), out_shape=out_shap...]
where the time goes in v10:
time: 33.5 us; the launch traced here: 33.4 us
  Pallas kernels  32.7 us (98%)
  between operations  0.64 us (2%)
    pallas_call x1, Pallas kernels, per_device(): pl.pallas_call(functools.partial(kernel, total_steps), out_shape=out_shap...  32 us
    pallas_call x1, Pallas kernels, per_device(): pl.pallas_call(emit, out_shape=out_shape, in_specs=[vmem] * 4, out_specs=...  0.74 us

profile of v10, /device:TPU:64, one launch (start us, length us, event | category | flops | bytes accessed | tf_op | source)
XLA Modules:
  0.0 33.4 jit_solution(52400742278938798)
XLA Ops:
  0.6 32.0 %shard_map.75 = (bf16[64,1024]{1,0:T(8,128)(2,1)S(1)}, f32[8,4096]{1,0:T(8,128)S(1)}, f32[32,128]{1,0:T(8,128)S(1)}, f32[1,64]{1,0:T(1,128)S(1)}) custom-call(bf16[1024,512]{1,0:T(8,128)(2,1)} %rec_hbm.1, bf16[3,1536,512]{2,1,0:T(8,128)(2,1)} %bitcast.5, f32[3,512]{1,0:T(4,128)} %bias_hbm.1, bf16[64,512]{1,0:T(8,128)(2,1)} %bitcast.6), custom_call_target="tpu_custom_call" | custom-call | tf_op jit(solution)/shard_map/pallas_call | solution.py:538
  32.6 0.7 %shard_map.76 = (bf16[64,1024]{1,0:T(8,128)(2,1)}, f32[8,4096]{1,0:T(8,128)}, f32[32,128]{1,0:T(8,128)}, f32[1,64]{1,0:T(1,128)}) custom-call(bf16[64,1024]{1,0:T(8,128)(2,1)S(1)} %get-tuple-element.12.refs_0_, f32[8,4096]{1,0:T(8,128)S(1)} %get-tuple-element.13.refs_1_, f32[32,128]{1,0:T(8,128)S(1)} %get-tuple-element.14.refs_2_, ...), custom_call_target="tpu_custom_call" | custom-call | tf_op jit(solution)/shard_map/pallas_call | solution.py:584

commit v11 on v9

--- a/solution.py
+++ b/solution.py
@@ -333,20 +333,23 @@
             add_level2(at % 4, columns)
             add_rows(512, my_rows, at % 4, columns)
 
-    steps = [(0, t) for t in range(4)]
-    for group in ((0, 1), (2,)):
-        for t in group:
-            for slot in range(1, 4):
-                wait_tile(slot, t)
-        everything(steps + [(slot, t) for t in group for slot in range(1, 4)])
-        steps = []
-    for slot in range(1, 4):
-        wait_tile(slot, 3)
-    for slot in range(1, 4):
-        prepare(slot, 3, slot)
-        columns = step_columns(slot)
-        add_rows(0, their_rows, slot, columns)
-        add_level2(slot, columns)
+    for t in range(2):
+        for slot in range(1, 4):
+            wait_tile(slot, t)
+    everything(
+        [(0, t) for t in range(4)] + [(slot, t) for t in range(2) for slot in range(1, 4)]
+    )
+    for t in (2, 3):
+        wait_tile(1, t)
+        wait_tile(2, t)
+        everything([(1, t), (2, t)])
+    wait_tile(3, 2)
+    everything([(3, 2)])
+    wait_tile(3, 3)
+    prepare(3, 3, 3)
+    last_columns = step_columns(3)
+    add_rows(0, their_rows, 3, last_columns)
+    add_level2(3, last_columns)
 
     low_half = lax.broadcasted_iota(jnp.int32, (64, 128), 1) < 64
 
@@ -384,8 +387,7 @@
     swap = remote(partner_out, partner_in, p_send, p_recv, partner)
     swap.start()
 
-    for slot in range(1, 4):
-        add_rows(512, my_rows, slot, step_columns(slot))
+    add_rows(512, my_rows, 3, step_columns(3))
     third_rows(512, my_rows, mine)
     low_levels(mine)
     swap.wait_recv()

time: 32.7 us -> 33.1 us (1.012)
  no operation moved by 1% of the time
where the time goes in v11:
time: 33.1 us; the launch traced here: 32.8 us
  Pallas kernels  32.1 us (97%)
  between operations  0.64 us (2%)
    pallas_call x1, Pallas kernels, per_device(): pl.pallas_call(functools.partial(kernel, total_steps), out_shape=out_shap...  31.4 us
    pallas_call x1, Pallas kernels, per_device(): pl.pallas_call(emit, out_shape=out_shape, in_specs=[vmem] * 4, out_specs=...  0.74 us

profile of v11, /device:TPU:64, one launch (start us, length us, event | category | flops | bytes accessed | tf_op | source)
XLA Modules:
  0.0 32.8 jit_solution(3518222007090095967)
XLA Ops:
  0.6 31.4 %shard_map.75 = (bf16[64,1024]{1,0:T(8,128)(2,1)S(1)}, f32[8,4096]{1,0:T(8,128)S(1)}, f32[32,128]{1,0:T(8,128)S(1)}, f32[1,64]{1,0:T(1,128)S(1)}) custom-call(bf16[1024,512]{1,0:T(8,128)(2,1)} %rec_hbm.1, bf16[3,1536,512]{2,1,0:T(8,128)(2,1)} %bitcast.5, f32[3,512]{1,0:T(4,128)} %bias_hbm.1, bf16[64,512]{1,0:T(8,128)(2,1)} %bitcast.6), custom_call_target="tpu_custom_call" | custom-call | tf_op jit(solution)/shard_map/pallas_call | solution.py:540
  32.0 0.7 %shard_map.76 = (bf16[64,1024]{1,0:T(8,128)(2,1)}, f32[8,4096]{1,0:T(8,128)}, f32[32,128]{1,0:T(8,128)}, f32[1,64]{1,0:T(1,128)}) custom-call(bf16[64,1024]{1,0:T(8,128)(2,1)S(1)} %get-tuple-element.12.refs_0_, f32[8,4096]{1,0:T(8,128)S(1)} %get-tuple-element.13.refs_1_, f32[32,128]{1,0:T(8,128)S(1)} %get-tuple-element.14.refs_2_, ...), custom_call_target="tpu_custom_call" | custom-call | tf_op jit(solution)/shard_map/pallas_call | solution.py:586
